TPU v7x, 32 devices: a whole 2x2x4 slice. The times are simulated.
32 devices in a mesh: groups: 2 (over x), mem: 16 (over z, y, core).
Axes of the slice: x: 2, y: 2, z: 4, core: 2. Of those that a mesh axis runs over, the one named last changes fastest.
Arguments:
- mem_key: bfloat16 [128, 128, 128], P(('groups', 'mem')), parts along dimension 0, may hold values from -6 to 6
- value_base: bfloat16 [128, 128, 512], P(('groups', 'mem')), parts along dimension 0, may hold values from -6 to 6
- memory_labels: int32 [128, 128], P(('groups', 'mem')), parts along dimension 0, may hold values from 0 to 7
- valid_counts: int32 [32], P(('groups', 'mem')), parts along dimension 0, may hold values from 128 to 512, as said below
- query_key: bfloat16 [32, 64, 128], P(('groups', 'mem')), parts along dimension 0, may hold values from -96 to 96
- query_value: bfloat16 [32, 64, 512], P(('groups', 'mem')), parts along dimension 0, may hold values from -6 to 6
- object_embed: bfloat16 [8, 512], replicated, may hold values from -6 to 6
- decode_weight: bfloat16 [3, 3, 1024, 256], replicated, may hold values from -0.0625 to 0.0625
- mask_weight: bfloat16 [256, 8], replicated, may hold values from -0.375 to 0.375
Outputs:
- mask_logits: float32 [32, 64, 8], P(('groups', 'mem')), parts along dimension 0
There are 2 independent parts, one for each index of `groups`. A program takes and returns all parts, laid end to end along the dimension named above; an argument that names none is the same for every part. Nothing has to cross between parts.
Inputs may be any that keep to these rules, and one draw needn't show every extreme that they name: `valid_counts`: live positions of each memory block; some block is full and some holds a quarter.
All inputs are finite; a program needn't handle non-finite values.
Results may differ from a plain program's by a relative error of at most 0.0048.
Values may be sent and summed in bfloat16 or wider, within the bound.
No kernel may reach another device: no remote copies, remote signals or barrier semaphores. Data moves between devices by JAX's collectives and lax.ppermute only.
A program may use at most 320 MiB of HBM per device.

v0:
```python
import functools
import math

import jax
import jax.numpy as jnp
from jax import lax
from jax.experimental import pallas as pl
from jax.experimental.pallas import tpu as pltpu
from jax.sharding import PartitionSpec as P


F32 = jnp.float32
BF16 = jnp.bfloat16
PAD = 16
VM = pl.BlockSpec(memory_space=pltpu.VMEM)
SM = pl.BlockSpec(memory_space=pltpu.SMEM)
HB = pl.BlockSpec(memory_space=pl.ANY)
S = jax.ShapeDtypeStruct


def call(kernel, out, ins, far=(), scratch=(), flops=0, exps=0, grant=24):
    size = lambda a: math.prod(a.shape) * jnp.dtype(a.dtype).itemsize
    outs = out if isinstance(out, (tuple, list)) else (out,)
    moved = sum(size(a) for a in ins) + sum(size(a) for a in outs)
    small = lambda a: a.ndim == 1 and a.dtype == jnp.int32
    return pl.pallas_call(
        kernel,
        out_shape=out,
        in_specs=[HB if i in far else SM if small(a) else VM for i, a in enumerate(ins)],
        out_specs=jax.tree.map(lambda _: VM, out),
        scratch_shapes=scratch,
        cost_estimate=pl.CostEstimate(flops=flops, transcendentals=exps, bytes_accessed=moved),
        compiler_params=pltpu.CompilerParams(vmem_limit_bytes=int(grant * 2**20)),
    )(*ins)


def prep_kernel(
    count_ref, key_hbm, val_hbm, lab_hbm, emb_hbm, out_ref,
    key_ref, val_ref, lab_ref, emb_ref, sems,
):
    copies = [
        pltpu.make_async_copy(src, dst, sems.at[i])
        for i, (src, dst) in enumerate(
            (
                (val_hbm, val_ref),
                (key_hbm, key_ref),
                (lab_hbm, lab_ref),
                (emb_hbm, emb_ref),
            )
        )
    ]
    for copy in copies:
        copy.start()
    pos, width = val_ref.shape
    kwidth = key_ref.shape[1]
    count = count_ref[0]
    chunk = lab_ref.shape[1]
    objects = emb_ref.shape[0]
    out_ref[...] = jnp.zeros_like(out_ref)
    for copy in copies:
        copy.wait()
    live_row = lax.broadcasted_iota(jnp.int32, (pos, kwidth), 0) < count
    keys = key_ref[...].astype(F32)
    keys = jnp.where(live_row, keys, jnp.broadcast_to(keys[0:1], keys.shape))
    out_ref[0:pos, pos : pos + kwidth] = keys.astype(BF16)
    for i in range(pos // chunk):
        ids = jnp.broadcast_to(lab_ref[i : i + 1, :], (objects, chunk))
        onehot = (ids == lax.broadcasted_iota(jnp.int32, (objects, chunk), 0)).astype(F32)
        embedded = lax.dot_general(
            emb_ref[...].astype(F32), onehot, (((0,), (0,)), ((), ())), preferred_element_type=F32
        )
        value = val_ref[i * chunk : (i + 1) * chunk, :].astype(F32).T + embedded
        lane = lax.broadcasted_iota(jnp.int32, (width, chunk), 1) + i * chunk
        value = jnp.where(lane < count, value, 0.0)
        out_ref[0:width, i * chunk : (i + 1) * chunk] = value.astype(BF16)
        tail = lax.broadcasted_iota(jnp.int32, (PAD, chunk), 0)
        lane = lax.broadcasted_iota(jnp.int32, (PAD, chunk), 1) + i * chunk
        out_ref[width : width + PAD, i * chunk : (i + 1) * chunk] = jnp.where(
            (tail == 0) & (lane < count), 1.0, 0.0
        ).astype(BF16)


def pack_tail(peak, mass):
    row = lax.broadcasted_iota(jnp.int32, (PAD, peak.shape[1]), 0)
    high = mass.astype(BF16).astype(F32)
    low = mass - high
    out = jnp.where(row == 0, peak, jnp.where(row == 1, high, jnp.where(row == 2, low, 0.0)))
    return out.astype(BF16)


def keep_tail(peak, mass):
    row = lax.broadcasted_iota(jnp.int32, (PAD, peak.shape[1]), 0)
    return jnp.where(row == 0, peak, jnp.where(row == 1, mass, 0.0))


def attend(blocks, queries, pos, kwidth, width):
    scale = 1.0 / math.sqrt(kwidth)
    parts = []
    for ref in blocks:
        keys = ref[0:pos, pos : pos + kwidth]
        scores = (
            lax.dot_general(keys, queries, (((1,), (1,)), ((), ())), preferred_element_type=F32)
            * scale
        )
        peak = jnp.max(scores, axis=0, keepdims=True)
        weights = jnp.exp(scores - peak).astype(BF16)
        values = jnp.dot(ref[0 : width + PAD, 0:pos], weights, preferred_element_type=F32)
        parts.append((peak, values))
    (peak0, values0), (peak1, values1) = parts
    peak = jnp.maximum(peak0, peak1).astype(BF16).astype(F32)
    values = values0 * jnp.exp(peak0 - peak) + values1 * jnp.exp(peak1 - peak)
    return peak, values


def attend_kernel(pos, kwidth, width, send, mine_ref, other_ref, q_ref, out_ref):
    peak, values = attend((mine_ref, other_ref), q_ref[...], pos, kwidth, width)
    mass = values[width : width + 1]
    out_ref[0:width] = values[0:width].astype(out_ref.dtype)
    out_ref[width : width + PAD] = (pack_tail if send else keep_tail)(peak, mass)


def merged(width, keep_ref, got_ref):
    got_peak = got_ref[width : width + PAD].astype(F32)
    peak, mass = keep_ref[width : width + 1], keep_ref[width + 1 : width + 2]
    got_mass = got_peak[1:2] + got_peak[2:3]
    got_peak = got_peak[0:1]
    top = jnp.maximum(peak, got_peak)
    a, b = jnp.exp(peak - top), jnp.exp(got_peak - top)
    values = keep_ref[0:width] * a + got_ref[0:width].astype(F32) * b
    return values, top, mass * a + got_mass * b


def fold_kernel(width, keep_ref, got_ref, send_out, keep_out):
    values, peak, mass = merged(width, keep_ref, got_ref)
    half = values.shape[1] // 2
    if half % 128 == 0:
        send_out[0:width] = values[:, half:].astype(BF16)
        send_out[width : width + PAD] = pack_tail(peak[:, half:], mass[:, half:])
        keep_out[0:width] = values[:, :half]
        keep_out[width : width + PAD] = keep_tail(peak[:, :half], mass[:, :half])
        return
    rows = width // 2
    low, high = values[0:rows], values[rows:]
    lane = lax.broadcasted_iota(jnp.int32, (1, 2 * half), 1) < half
    swap = lambda x: pltpu.roll(x, half, 1)
    first = lambda x: jnp.where(lane, x, swap(x))
    second = lambda x: jnp.where(lane, swap(x), x)
    peak8, mass8 = (jnp.broadcast_to(x, (8, 2 * half)) for x in (peak, mass))
    send_out[0:rows] = jnp.where(lane, swap(low), high).astype(BF16)
    send_out[rows : rows + PAD] = pack_tail(second(peak8)[0:1], second(mass8)[0:1])
    keep_out[0:rows] = jnp.where(lane, low, swap(high))
    keep_out[rows : rows + PAD] = keep_tail(first(peak8)[0:1], first(mass8)[0:1])


def readout_kernel(rows, keep_ref, got_ref, frame_ref, out_ref):
    values, _, mass = merged(rows, keep_ref, got_ref)
    turned = (values / mass).T
    half = turned.shape[0] // 2
    out_ref[:, 0:rows] = turned[0:half].astype(BF16)
    out_ref[:, rows : 2 * rows] = turned[half:].astype(BF16)
    out_ref[:, 2 * rows :] = frame_ref[...]


def join_kernel(a_ref, b_ref, out_ref):
    rows = a_ref.shape[0]
    out_ref[0:rows] = a_ref[...]
    out_ref[rows:] = b_ref[...]


def slide(left, right):
    rows = left.shape[0]
    row = lax.broadcasted_iota(jnp.int32, left.shape, 0)
    left = jnp.where(row == 0, 0.0, pltpu.roll(left, 1, 0))
    right = jnp.where(row == rows - 1, 0.0, pltpu.roll(right, rows - 1, 0))
    return left + right


def taps(lines):
    total = []
    for col in range(3):
        acc = None
        for line, weight in lines:
            term = jnp.dot(line, weight(col), preferred_element_type=F32)
            acc = term if acc is None else acc + term
        total.append(acc)
    return slide(total[0], total[2]) + total[1]


def ends(odd_ref, near_ref, far_ref):
    odd = odd_ref[0] == 1
    near, far = near_ref[...], far_ref[...]
    return jnp.where(odd, near, far), jnp.where(odd, far, near)


def mid_conv_kernel(mid_ref, w_hbm, out_ref, ends_ref, w_ref, sems):
    pairs = (
        (w_hbm.at[1], w_ref),
        (w_hbm.at[0], ends_ref.at[0]),
        (w_hbm.at[2], ends_ref.at[1]),
    )
    copies = [pltpu.make_async_copy(a, b, sems.at[i]) for i, (a, b) in enumerate(pairs)]
    for copy in copies:
        copy.start()
    copies[0].wait()
    out_ref[...] = taps(((mid_ref[...], lambda col: w_ref[col]),))
    for copy in copies[1:]:
        copy.wait()


def last_kernel(odd_ref, sum_ref, near_ref, far_ref, w_ref, mask_ref, out_ref):
    up, down = ends(odd_ref, near_ref, far_ref)
    total = sum_ref[...] + taps(
        ((up, lambda col: w_ref[0, col]), (down, lambda col: w_ref[1, col]))
    )
    hidden = jnp.maximum(total, 0.0).astype(BF16)
    out_ref[...] = lax.dot_general(
        mask_ref[...], hidden, (((1,), (1,)), ((), ())), preferred_element_type=F32
    )


def shards(
    count,
    mem_key,
    value_base,
    memory_labels,
    valid_counts,
    query_key,
    query_value,
    object_embed,
    decode_weight,
    mask_weight,
):
    kwidth, width = mem_key.shape[2], value_base.shape[2]
    pos = mem_key.shape[0] * mem_key.shape[1]
    tall = max(pos, width) + PAD
    owned = query_value.shape[0] * query_value.shape[1]
    out_width = decode_weight.shape[3]

    def swap(x, mask):
        return lax.ppermute(x, "mem", [(i, i ^ mask) for i in range(count)])

    near_by = lambda x: swap(x, 1)
    links = [(i, i + 1) for i in range(1, count - 1, 2)]
    links = links + [(b, a) for a, b in links]
    far_by = lambda x: lax.ppermute(x, "mem", links)

    masks = [1 << i for i in range(1, count.bit_length() - 1)]
    if len(masks) > 1:
        masks[0], masks[1] = masks[1], masks[0]

    queries = query_key.reshape(owned, kwidth)
    frame = query_value.reshape(owned, width)
    odd = lax.bitwise_and(lax.axis_index("mem"), 1).reshape(1).astype(jnp.int32)

    dma = pltpu.SemaphoreType.DMA
    got = swap(queries, masks[-1])
    mine = call(
        prep_kernel,
        S((tall, pos + kwidth), BF16),
        (
            valid_counts,
            mem_key.reshape(pos, kwidth),
            value_base.reshape(pos, width),
            memory_labels,
            object_embed,
        ),
        far=(1, 2, 3, 4),
        scratch=(
            pltpu.VMEM((pos, kwidth), BF16),
            pltpu.VMEM((pos, width), BF16),
            pltpu.VMEM(memory_labels.shape, jnp.int32),
            pltpu.VMEM(object_embed.shape, BF16),
            dma((4,)),
        ),
        flops=2 * pos * width * 8,
        grant=58,
    )
    other = near_by(mine)

    for mask in masks[-2::-1]:
        queries = call(
            join_kernel, S((2 * queries.shape[0], kwidth), BF16), (queries, got)
        )
        got = swap(queries, mask)
    theirs = got

    lanes = queries.shape[0]
    work = dict(flops=4 * lanes * pos * (kwidth + width), exps=2 * lanes * pos)
    attend_call = lambda q, send, dtype: call(
        functools.partial(attend_kernel, pos, kwidth, width, send),
        S((width + PAD, lanes), dtype),
        (mine, other, q),
        **work,
    )
    keep = attend_call(queries, False, F32)
    send = attend_call(theirs, True, BF16)
    conv_flops = 2 * owned * width * out_width * 3
    rows = width
    for i, mask in enumerate(masks):
        got = swap(send, mask)
        if i + 1 == len(masks):
            break
        lanes = lanes // 2
        if lanes % 128:
            out_rows, out_lanes = rows // 2 + PAD, 2 * lanes
        else:
            out_rows, out_lanes = rows + PAD, lanes
        send, keep = call(
            functools.partial(fold_kernel, rows),
            (S((out_rows, out_lanes), BF16), S((out_rows, out_lanes), F32)),
            (keep, got),
            flops=3 * rows * lanes,
        )
        rows = out_rows - PAD
    joined = call(
        functools.partial(readout_kernel, rows),
        S((owned, 2 * width), BF16),
        (keep, got, frame),
        flops=3 * rows * lanes,
    )
    far = far_by(joined)
    near = near_by(joined)
    part, end_weight = call(
        mid_conv_kernel,
        (S((owned, out_width), F32), S((2, *decode_weight.shape[1:]), BF16)),
        (joined, decode_weight),
        far=(1,),
        scratch=(pltpu.VMEM(decode_weight.shape[1:], BF16), dma((3,))),
        flops=2 * conv_flops,
        grant=50,
    )
    objects = mask_weight.shape[1]
    logits = call(
        last_kernel,
        S((objects, owned), F32),
        (odd, part, near, far, end_weight, mask_weight.T),
        flops=4 * conv_flops,
    )
    return logits.T.reshape(query_value.shape[0], query_value.shape[1], objects)


def solution(mesh):
    split = P(("groups", "mem"))
    count = mesh.shape["mem"]

    def step(*args):
        return shards(count, *args)

    return jax.shard_map(
        step,
        mesh=mesh,
        in_specs=(split,) * 6 + (P(),) * 3,
        out_specs=split,
        check_vma=False,
    )
```

profile of v0, /device:TPU:25, one launch (start us, length us, event | category | flops | bytes accessed | tf_op | source)
XLA Modules:
  0.0 46.1 jit_solution(16397716182965804263)
XLA Ops:
  0.0 0.0 copy-start.1
  0.7 2.5 %shard_map.91.mine_ref = bf16[528,640]{1,0:T(8,128)(2,1)} custom-call(s32[1]{0:T(128)S(6)} %copy.10.count_ref, bf16[512,128]{1,0:T(8,128)(2,1)} %bitcast.14, bf16[512,512]{1,0:T(8,128)(2,1)} %bitcast.13, s32[4,128]{1,0:T(4,128)} %lab_hbm.1, bf16[8,512]{1,0:T(8,128)(2,1)} %emb_hbm.1), custom_call_target="tpu_custom_call" | custom-call | flops 4194304 | bytes 1341444 | tf_op jit(solution)/shard_map/pallas_call | solution.py:26
  3.1 0.7 %collective-permute-start = (bf16[528,640]{1,0:T(8,128)(2,1)}, bf16[528,640]{1,0:T(8,128)(2,1)S(1)}, u32[]{:S(2)}, u32[]{:S(2)}) collective-permute-start(bf16[528,640]{1,0:T(8,128)(2,1)} %shard_map.91.mine_ref), channel_id=1, source_target_pairs={{0,1},{1,0},{2,3},{3,2},{4,5},{5,4},{6,7},{7,6},{8,9},{9,8},{10,11... | collective-permute-start | bytes 2027528 | tf_op jit(solution)/shard_map/ppermute | solution.py:240
  3.9 0.1 collective-permute-start.1
  3.9 3.7 %collective-permute-done.1.b_ref = bf16[64,128]{1,0:T(8,128)(2,1)S(1)} collective-permute-done((bf16[64,128]{1,0:T(8,128)(2,1)}, bf16[64,128]{1,0:T(8,128)(2,1)S(1)}, u32[]{:S(2)}, u32[]{:S(2)}) %collective-permute-start.1) | collective-permute-done | bytes 16416 | tf_op jit(solution)/shard_map/ppermute | solution.py:240
  7.6 0.0 copy-start.2
  7.6 0.7 %copy-done.2 = bf16[1,64,128]{2,1,0:T(8,128)(2,1)S(1)} copy-done((bf16[1,64,128]{2,1,0:T(8,128)(2,1)S(1)}, bf16[1,64,128]{2,1,0:T(8,128)(2,1)}, u32[]{:S(2)}) %copy-start.2) | copy-done | bytes 16408
  8.4 1.2 %collective-permute-start.2 = (bf16[128,128]{1,0:T(8,128)(2,1)S(1)}, bf16[128,128]{1,0:T(8,128)(2,1)S(1)}, u32[]{:S(2)}, u32[]{:S(2)}) collective-permute-start(bf16[128,128]{1,0:T(8,128)(2,1)S(1)} %shard_map.92.a_ref), channel_id=1, source_target_pairs={{0,2},{1,3},{2,0},{3,1},{4,6},{5,7},{6,4},{7,5},{8,10},{9,11},{10,... | collective-permute-start | bytes 98312 | tf_op jit(solution)/shard_map/ppermute | solution.py:240
  9.6 1.5 %collective-permute-done.2.b_ref = bf16[128,128]{1,0:T(8,128)(2,1)S(1)} collective-permute-done((bf16[128,128]{1,0:T(8,128)(2,1)S(1)}, bf16[128,128]{1,0:T(8,128)(2,1)S(1)}, u32[]{:S(2)}, u32[]{:S(2)}) %collective-permute-start.2) | collective-permute-done | bytes 32800 | tf_op jit(solution)/shard_map/ppermute | solution.py:240
  11.1 0.0 copy-start.3
  11.1 0.2 collective-permute-start.3
  11.3 3.0 %collective-permute-done.3.q_ref = bf16[256,128]{1,0:T(8,128)(2,1)S(1)} collective-permute-done((bf16[256,128]{1,0:T(8,128)(2,1)S(1)}, bf16[256,128]{1,0:T(8,128)(2,1)S(1)}, u32[]{:S(2)}, u32[]{:S(2)}) %collective-permute-start.3) | collective-permute-done | bytes 65568 | tf_op jit(solution)/shard_map/ppermute | solution.py:240
  14.3 0.0 collective-permute-done.other_ref
  14.3 0.0 copy-start
  14.3 1.1 %copy-done = bf16[528,640]{1,0:T(8,128)(2,1)S(1)} copy-done((bf16[528,640]{1,0:T(8,128)(2,1)S(1)}, bf16[528,640]{1,0:T(8,128)(2,1)}, u32[]{:S(2)}) %copy-start) | copy-done | bytes 675864
  15.4 0.9 %shard_map.95 = bf16[528,256]{1,0:T(8,128)(2,1)S(1)} custom-call(bf16[528,640]{1,0:T(8,128)(2,1)S(1)} %copy-done, bf16[528,640]{1,0:T(8,128)(2,1)S(1)} %collective-permute-done.other_ref, bf16[256,128]{1,0:T(8,128)(2,1)S(1)} %collective-permute-done.3.q_ref), custom_call_target="tpu_custom_call" | custom-call | flops 335544320 | bytes 1687552 | tf_op jit(solution)/shard_map/pallas_call | solution.py:26
  16.3 0.2 collective-permute-start.4
  16.5 0.9 %shard_map.94.keep_ref = f32[528,256]{1,0:T(8,128)S(1)} custom-call(bf16[528,640]{1,0:T(8,128)(2,1)S(1)} %copy-done, bf16[528,640]{1,0:T(8,128)(2,1)S(1)} %collective-permute-done.other_ref, bf16[256,128]{1,0:T(8,128)(2,1)S(1)} %shard_map.93.q_ref), custom_call_target="tpu_custom_call" | custom-call | flops 335544320 | bytes 1957888 | tf_op jit(solution)/shard_map/pallas_call | solution.py:26
  17.4 4.3 %collective-permute-done.4.got_ref = bf16[528,256]{1,0:T(8,128)(2,1)S(1)} collective-permute-done((bf16[528,256]{1,0:T(8,128)(2,1)S(1)}, bf16[528,256]{1,0:T(8,128)(2,1)S(1)}, u32[]{:S(2)}, u32[]{:S(2)}) %collective-permute-start.4) | collective-permute-done | bytes 270368 | tf_op jit(solution)/shard_map/ppermute | solution.py:240
  21.7 0.1 shard_map.96
  21.8 1.3 %collective-permute-start.5 = (bf16[528,128]{1,0:T(8,128)(2,1)S(1)}, bf16[528,128]{1,0:T(8,128)(2,1)S(1)}, u32[]{:S(2)}, u32[]{:S(2)}) collective-permute-start(bf16[528,128]{1,0:T(8,128)(2,1)S(1)} %get-tuple-element.12), channel_id=1, source_target_pairs={{0,2},{1,3},{2,0},{3,1},{4,6},{5,7},{6,4},{7,5},{8,10},{9,11},{10,... | collective-permute-start | bytes 405512 | tf_op jit(solution)/shard_map/ppermute | solution.py:240
  23.1 2.9 %collective-permute-done.5.got_ref = bf16[528,128]{1,0:T(8,128)(2,1)S(1)} collective-permute-done((bf16[528,128]{1,0:T(8,128)(2,1)S(1)}, bf16[528,128]{1,0:T(8,128)(2,1)S(1)}, u32[]{:S(2)}, u32[]{:S(2)}) %collective-permute-start.5) | collective-permute-done | bytes 135200 | tf_op jit(solution)/shard_map/ppermute | solution.py:240
  26.0 0.1 shard_map.97
  26.1 0.1 collective-permute-start.6
  26.2 4.6 %collective-permute-done.6.got_ref = bf16[272,128]{1,0:T(8,128)(2,1)S(1)} collective-permute-done((bf16[272,128]{1,0:T(8,128)(2,1)S(1)}, bf16[272,128]{1,0:T(8,128)(2,1)S(1)}, u32[]{:S(2)}, u32[]{:S(2)}) %collective-permute-start.6) | collective-permute-done | bytes 69664 | tf_op jit(solution)/shard_map/ppermute | solution.py:240
  30.8 0.0 copy-done.1
  30.8 0.1 shard_map.98.mid_ref
  31.0 9.7 %collective-permute-start.8 = (bf16[64,1024]{1,0:T(8,128)(2,1)S(1)}, bf16[64,1024]{1,0:T(8,128)(2,1)S(1)}, u32[]{:S(2)}, u32[]{:S(2)}) collective-permute-start(bf16[64,1024]{1,0:T(8,128)(2,1)S(1)} %shard_map.98.mid_ref), channel_id=1, source_target_pairs={{1,2},{3,4},{5,6},{7,8},{9,10},{11,12},{13,14},{2,1},{4,3},{6,5},{... | collective-permute-start | bytes 393224 | tf_op jit(solution)/shard_map/ppermute | solution.py:245
  40.7 0.1 collective-permute-start.7
  40.8 2.4 %shard_map.99 = (f32[64,256]{1,0:T(8,128)S(1)}, bf16[2,3,1024,256]{3,2,1,0:T(8,128)(2,1)S(1)}) custom-call(bf16[64,1024]{1,0:T(8,128)(2,1)S(1)} %shard_map.98.mid_ref, bf16[3,3,1024,256]{3,2,1,0:T(8,128)(2,1)} %w_hbm.1), custom_call_target="tpu_custom_call" | custom-call | flops 100663296 | bytes 8060928 | tf_op jit(solution)/shard_map/pallas_call | solution.py:26
  43.2 1.6 %collective-permute-done.8.far_ref = bf16[64,1024]{1,0:T(8,128)(2,1)S(1)} collective-permute-done((bf16[64,1024]{1,0:T(8,128)(2,1)S(1)}, bf16[64,1024]{1,0:T(8,128)(2,1)S(1)}, u32[]{:S(2)}, u32[]{:S(2)}) %collective-permute-start.8) | collective-permute-done | bytes 131104 | tf_op jit(solution)/shard_map/ppermute | solution.py:245
  44.8 0.0 collective-permute-done.7.near_ref
  44.8 0.0 copy-done.3
  44.8 1.4 %shard_map.100 = f32[8,64]{1,0:T(8,128)} custom-call(s32[1]{0:T(128)} %bitcast.odd_ref, f32[64,256]{1,0:T(8,128)S(1)} %get-tuple-element.15.sum_ref, bf16[64,1024]{1,0:T(8,128)(2,1)S(1)} %collective-permute-done.7.near_ref, bf16[64,1024]{1,0:T(8,128)(2,1)S(1)} %collective-permute-done.8.far_ref, bf16[2,3,1024,256]{3,2,1,0:T(8,128)(2,1)S(1)} %get-tuple-element.16.w_ref, ...), custom_call_target="tpu_custom_call" | custom-call | flops 201326592 | bytes 3479556 | tf_op jit(solution)/shard_map/pallas_call | solution.py:26
  (2 shorter events, 0.0 us)
Async XLA Ops:
  0.0 30.8 %copy-start.1 = (bf16[1,64,512]{2,1,0:T(8,128)(2,1)S(1)}, bf16[1,64,512]{2,1,0:T(8,128)(2,1)}, u32[]{:S(2)}) copy-start(bf16[1,64,512]{2,1,0:T(8,128)(2,1)} %param.14) | copy-start | bytes 196612
  3.1 11.2 %collective-permute-start = (bf16[528,640]{1,0:T(8,128)(2,1)}, bf16[528,640]{1,0:T(8,128)(2,1)S(1)}, u32[]{:S(2)}, u32[]{:S(2)}) collective-permute-start(bf16[528,640]{1,0:T(8,128)(2,1)} %shard_map.91.mine_ref), channel_id=1, source_target_pairs={{0,1},{1,0},{2,3},{3,2},{4,5},{5,4},{6,7},{7,6},{8,9},{9,8},{10,11... | collective-permute-start | bytes 2027528 | tf_op jit(solution)/shard_map/ppermute | solution.py:240
  3.9 3.8 %collective-permute-start.1 = (bf16[64,128]{1,0:T(8,128)(2,1)}, bf16[64,128]{1,0:T(8,128)(2,1)S(1)}, u32[]{:S(2)}, u32[]{:S(2)}) collective-permute-start(bf16[64,128]{1,0:T(8,128)(2,1)} %bitcast.10), channel_id=1, source_target_pairs={{0,8},{1,9},{2,10},{3,11},{4,12},{5,13},{6,14},{7,15},{8,0},{9,1},... | collective-permute-start | bytes 49160 | tf_op jit(solution)/shard_map/ppermute | solution.py:240
  7.6 0.7 %copy-start.2 = (bf16[1,64,128]{2,1,0:T(8,128)(2,1)S(1)}, bf16[1,64,128]{2,1,0:T(8,128)(2,1)}, u32[]{:S(2)}) copy-start(bf16[1,64,128]{2,1,0:T(8,128)(2,1)} %param.13) | copy-start | bytes 49156
  8.4 2.8 %collective-permute-start.2 = (bf16[128,128]{1,0:T(8,128)(2,1)S(1)}, bf16[128,128]{1,0:T(8,128)(2,1)S(1)}, u32[]{:S(2)}, u32[]{:S(2)}) collective-permute-start(bf16[128,128]{1,0:T(8,128)(2,1)S(1)} %shard_map.92.a_ref), channel_id=1, source_target_pairs={{0,2},{1,3},{2,0},{3,1},{4,6},{5,7},{6,4},{7,5},{8,10},{9,11},{10,... | collective-permute-start | bytes 98312 | tf_op jit(solution)/shard_map/ppermute | solution.py:240
  11.1 33.6 %copy-start.3 = (bf16[256,8]{0,1:T(8,128)(2,1)S(1)}, bf16[256,8]{0,1:T(8,128)(2,1)}, u32[]{:S(2)}) copy-start(bf16[256,8]{0,1:T(8,128)(2,1)} %param.17) | copy-start | bytes 12292
  11.1 3.2 %collective-permute-start.3 = (bf16[256,128]{1,0:T(8,128)(2,1)S(1)}, bf16[256,128]{1,0:T(8,128)(2,1)S(1)}, u32[]{:S(2)}, u32[]{:S(2)}) collective-permute-start(bf16[256,128]{1,0:T(8,128)(2,1)S(1)} %shard_map.93.q_ref), channel_id=1, source_target_pairs={{0,4},{1,5},{2,6},{3,7},{4,0},{5,1},{6,2},{7,3},{8,12},{9,13},{10,... | collective-permute-start | bytes 196616 | tf_op jit(solution)/shard_map/ppermute | solution.py:240
  14.3 1.1 %copy-start = (bf16[528,640]{1,0:T(8,128)(2,1)S(1)}, bf16[528,640]{1,0:T(8,128)(2,1)}, u32[]{:S(2)}) copy-start(bf16[528,640]{1,0:T(8,128)(2,1)} %shard_map.91.mine_ref) | copy-start | bytes 2027524
  16.3 5.4 %collective-permute-start.4 = (bf16[528,256]{1,0:T(8,128)(2,1)S(1)}, bf16[528,256]{1,0:T(8,128)(2,1)S(1)}, u32[]{:S(2)}, u32[]{:S(2)}) collective-permute-start(bf16[528,256]{1,0:T(8,128)(2,1)S(1)} %shard_map.95), channel_id=1, source_target_pairs={{0,4},{1,5},{2,6},{3,7},{4,0},{5,1},{6,2},{7,3},{8,12},{9,13},{10,... | collective-permute-start | bytes 811016 | tf_op jit(solution)/shard_map/ppermute | solution.py:240
  21.8 4.2 %collective-permute-start.5 = (bf16[528,128]{1,0:T(8,128)(2,1)S(1)}, bf16[528,128]{1,0:T(8,128)(2,1)S(1)}, u32[]{:S(2)}, u32[]{:S(2)}) collective-permute-start(bf16[528,128]{1,0:T(8,128)(2,1)S(1)} %get-tuple-element.12), channel_id=1, source_target_pairs={{0,2},{1,3},{2,0},{3,1},{4,6},{5,7},{6,4},{7,5},{8,10},{9,11},{10,... | collective-permute-start | bytes 405512 | tf_op jit(solution)/shard_map/ppermute | solution.py:240
  26.1 4.7 %collective-permute-start.6 = (bf16[272,128]{1,0:T(8,128)(2,1)S(1)}, bf16[272,128]{1,0:T(8,128)(2,1)S(1)}, u32[]{:S(2)}, u32[]{:S(2)}) collective-permute-start(bf16[272,128]{1,0:T(8,128)(2,1)S(1)} %get-tuple-element.14), channel_id=1, source_target_pairs={{0,8},{1,9},{2,10},{3,11},{4,12},{5,13},{6,14},{7,15},{8,0},{9,1},... | collective-permute-start | bytes 208904 | tf_op jit(solution)/shard_map/ppermute | solution.py:240
  31.0 13.8 %collective-permute-start.8 = (bf16[64,1024]{1,0:T(8,128)(2,1)S(1)}, bf16[64,1024]{1,0:T(8,128)(2,1)S(1)}, u32[]{:S(2)}, u32[]{:S(2)}) collective-permute-start(bf16[64,1024]{1,0:T(8,128)(2,1)S(1)} %shard_map.98.mid_ref), channel_id=1, source_target_pairs={{1,2},{3,4},{5,6},{7,8},{9,10},{11,12},{13,14},{2,1},{4,3},{6,5},{... | collective-permute-start | bytes 393224 | tf_op jit(solution)/shard_map/ppermute | solution.py:245
  40.7 4.0 %collective-permute-start.7 = (bf16[64,1024]{1,0:T(8,128)(2,1)S(1)}, bf16[64,1024]{1,0:T(8,128)(2,1)S(1)}, u32[]{:S(2)}, u32[]{:S(2)}) collective-permute-start(bf16[64,1024]{1,0:T(8,128)(2,1)S(1)} %shard_map.98.mid_ref), channel_id=1, source_target_pairs={{0,1},{1,0},{2,3},{3,2},{4,5},{5,4},{6,7},{7,6},{8,9},{9,8},{10,11... | collective-permute-start | bytes 393224 | tf_op jit(solution)/shard_map/ppermute | solution.py:240
where the time goes:
time: 46.4 us; the launch traced here: 46.1 us
  waiting for transfers between devices  21.6 us (47%)
  starting transfers between devices  13.6 us (29%)
  Pallas kernels  8.35 us (18%)
  local copies, waits for them, and re-layouts  1.82 us (4%)
  between operations  0.78 us (2%)
    ppermute x8, waiting for transfers between devices, swap(): return lax.ppermute(x, 'mem', [(i, i ^ mask) for i in range(count)])  20 us
    ppermute x1, starting transfers between devices, shards(): far_by = lambda x: lax.ppermute(x, 'mem', links)  9.75 us
    pallas_call x10, Pallas kernels, call(): pl.pallas_call(kernel, out_shape=out, in_specs=[HB if i in far else SM if...  8.35 us
    ppermute x8, starting transfers between devices, swap(): return lax.ppermute(x, 'mem', [(i, i ^ mask) for i in range(count)])  3.85 us
    unnamed x8, local copies, waits for them, and re-layouts  1.82 us
    ppermute x1, waiting for transfers between devices, shards(): far_by = lambda x: lax.ppermute(x, 'mem', links)  1.57 us
  transfers between devices with their start and end apart: 9, of which 7 were waited for; matrix products, arithmetic and copies ran while one was open for 0% of the time, Pallas kernels for 7%

commit v1 on v0

--- a/solution.py
+++ b/solution.py
@@ -16,9 +16,10 @@
 SM = pl.BlockSpec(memory_space=pltpu.SMEM)
 HB = pl.BlockSpec(memory_space=pl.ANY)
 S = jax.ShapeDtypeStruct
-
-
-def call(kernel, out, ins, far=(), scratch=(), flops=0, exps=0, grant=24):
+hold = pltpu.with_memory_space_constraint
+
+
+def call(kernel, out, ins, far=(), scratch=(), flops=0, exps=0):
     size = lambda a: math.prod(a.shape) * jnp.dtype(a.dtype).itemsize
     outs = out if isinstance(out, (tuple, list)) else (out,)
     moved = sum(size(a) for a in ins) + sum(size(a) for a in outs)
@@ -30,35 +31,32 @@
         out_specs=jax.tree.map(lambda _: VM, out),
         scratch_shapes=scratch,
         cost_estimate=pl.CostEstimate(flops=flops, transcendentals=exps, bytes_accessed=moved),
-        compiler_params=pltpu.CompilerParams(vmem_limit_bytes=int(grant * 2**20)),
-    )(*ins)
+        compiler_params=pltpu.CompilerParams(vmem_limit_bytes=24 << 20),
+    )(*[hold(a, pltpu.HBM) if i in far else a for i, a in enumerate(ins)])
 
 
 def prep_kernel(
-    count_ref, key_hbm, val_hbm, lab_hbm, emb_hbm, out_ref,
+    key_hbm, val_hbm, lab_hbm, emb_hbm, q_hbm, count_ref, out_ref, q_ref,
     key_ref, val_ref, lab_ref, emb_ref, sems,
 ):
-    copies = [
-        pltpu.make_async_copy(src, dst, sems.at[i])
-        for i, (src, dst) in enumerate(
-            (
-                (val_hbm, val_ref),
-                (key_hbm, key_ref),
-                (lab_hbm, lab_ref),
-                (emb_hbm, emb_ref),
-            )
-        )
-    ]
+    pairs = (
+        (val_hbm, val_ref),
+        (key_hbm, key_ref),
+        (lab_hbm, lab_ref),
+        (emb_hbm, emb_ref),
+        (q_hbm, q_ref),
+    )
+    copies = [pltpu.make_async_copy(a, b, sems.at[i]) for i, (a, b) in enumerate(pairs)]
     for copy in copies:
         copy.start()
     pos, width = val_ref.shape
     kwidth = key_ref.shape[1]
-    count = count_ref[0]
     chunk = lab_ref.shape[1]
     objects = emb_ref.shape[0]
     out_ref[...] = jnp.zeros_like(out_ref)
     for copy in copies:
         copy.wait()
+    count = count_ref[0]
     live_row = lax.broadcasted_iota(jnp.int32, (pos, kwidth), 0) < count
     keys = key_ref[...].astype(F32)
     keys = jnp.where(live_row, keys, jnp.broadcast_to(keys[0:1], keys.shape))
@@ -186,29 +184,39 @@
     return slide(total[0], total[2]) + total[1]
 
 
-def ends(odd_ref, near_ref, far_ref):
-    odd = odd_ref[0] == 1
+def ends(count, near_ref, far_ref):
+    place = lax.axis_index("mem")
+    odd = lax.rem(place, 2) == 1
     near, far = near_ref[...], far_ref[...]
+    far = jnp.where((place == 0) | (place == count - 1), jnp.zeros_like(far), far)
     return jnp.where(odd, near, far), jnp.where(odd, far, near)
 
 
-def mid_conv_kernel(mid_ref, w_hbm, out_ref, ends_ref, w_ref, sems):
-    pairs = (
-        (w_hbm.at[1], w_ref),
-        (w_hbm.at[0], ends_ref.at[0]),
-        (w_hbm.at[2], ends_ref.at[1]),
-    )
+def copy_all(pairs, sems):
     copies = [pltpu.make_async_copy(a, b, sems.at[i]) for i, (a, b) in enumerate(pairs)]
     for copy in copies:
         copy.start()
-    copies[0].wait()
+    return copies
+
+
+def stage_kernel(w_hbm, frame_hbm, ends_ref, frame_ref, sems):
+    pairs = (
+        (frame_hbm, frame_ref),
+        (w_hbm.at[0], ends_ref.at[0]),
+        (w_hbm.at[2], ends_ref.at[1]),
+    )
+    for copy in copy_all(pairs, sems):
+        copy.wait()
+
+
+def mid_conv_kernel(mid_ref, w_hbm, out_ref, w_ref, sems):
+    for copy in copy_all(((w_hbm.at[1], w_ref),), sems):
+        copy.wait()
     out_ref[...] = taps(((mid_ref[...], lambda col: w_ref[col]),))
-    for copy in copies[1:]:
-        copy.wait()
-
-
-def last_kernel(odd_ref, sum_ref, near_ref, far_ref, w_ref, mask_ref, out_ref):
-    up, down = ends(odd_ref, near_ref, far_ref)
+
+
+def last_kernel(count, sum_ref, near_ref, far_ref, w_ref, mask_ref, out_ref):
+    up, down = ends(count, near_ref, far_ref)
     total = sum_ref[...] + taps(
         ((up, lambda col: w_ref[0, col]), (down, lambda col: w_ref[1, col]))
     )
@@ -219,6 +227,7 @@
 
 
 def shards(
+    groups,
     count,
     mem_key,
     value_base,
@@ -236,52 +245,58 @@
     owned = query_value.shape[0] * query_value.shape[1]
     out_width = decode_weight.shape[3]
 
-    def swap(x, mask):
-        return lax.ppermute(x, "mem", [(i, i ^ mask) for i in range(count)])
-
-    near_by = lambda x: swap(x, 1)
-    links = [(i, i + 1) for i in range(1, count - 1, 2)]
-    links = links + [(b, a) for a, b in links]
-    far_by = lambda x: lax.ppermute(x, "mem", links)
-
-    masks = [1 << i for i in range(1, count.bit_length() - 1)]
-    if len(masks) > 1:
-        masks[0], masks[1] = masks[1], masks[0]
+    steps = count.bit_length() - 2
+    order = [[1 << i for i in range(1, steps + 1)] for _ in range(2)]
+    order[1][0:2] = order[1][1::-1]
+
+    def swap(x, step):
+        return lax.ppermute(x, "mem", [(i, i ^ order[i & 1][step]) for i in range(count)])
+
+    def near_by(x):
+        return lax.ppermute(x, "mem", [(i, i ^ 1) for i in range(count)])
+
+    def far_by(x):
+        links = []
+        for group in range(groups):
+            base = group * count
+            links += [(base + i, base + i + 1) for i in range(1, count - 1, 2)]
+            if groups % 2 == 0 and group % 2 == 0:
+                links += [(base + i, base + count + i) for i in (0, count - 1)]
+        links += [(b, a) for a, b in links]
+        return lax.ppermute(x, ("groups", "mem"), links)
 
     queries = query_key.reshape(owned, kwidth)
     frame = query_value.reshape(owned, width)
-    odd = lax.bitwise_and(lax.axis_index("mem"), 1).reshape(1).astype(jnp.int32)
-
     dma = pltpu.SemaphoreType.DMA
-    got = swap(queries, masks[-1])
-    mine = call(
+    got = swap(queries, steps - 1)
+    mine, queries = call(
         prep_kernel,
-        S((tall, pos + kwidth), BF16),
+        (S((tall, pos + kwidth), BF16), S(queries.shape, BF16)),
         (
-            valid_counts,
             mem_key.reshape(pos, kwidth),
             value_base.reshape(pos, width),
             memory_labels,
             object_embed,
+            queries,
+            valid_counts,
         ),
-        far=(1, 2, 3, 4),
+        far=range(5),
         scratch=(
             pltpu.VMEM((pos, kwidth), BF16),
             pltpu.VMEM((pos, width), BF16),
             pltpu.VMEM(memory_labels.shape, jnp.int32),
             pltpu.VMEM(object_embed.shape, BF16),
-            dma((4,)),
+            dma((5,)),
         ),
         flops=2 * pos * width * 8,
-        grant=58,
     )
     other = near_by(mine)
 
-    for mask in masks[-2::-1]:
+    for i in range(steps - 1):
         queries = call(
             join_kernel, S((2 * queries.shape[0], kwidth), BF16), (queries, got)
         )
-        got = swap(queries, mask)
+        got = swap(queries, steps - 2 - i)
     theirs = got
 
     lanes = queries.shape[0]
@@ -295,10 +310,18 @@
     keep = attend_call(queries, False, F32)
     send = attend_call(theirs, True, BF16)
     conv_flops = 2 * owned * width * out_width * 3
+    taps_shape = decode_weight.shape[1:]
+    end_weight, held = call(
+        stage_kernel,
+        (S((2, *taps_shape), BF16), S(frame.shape, BF16)),
+        (decode_weight, frame),
+        far=(0, 1),
+        scratch=(dma((3,)),),
+    )
     rows = width
-    for i, mask in enumerate(masks):
-        got = swap(send, mask)
-        if i + 1 == len(masks):
+    for i in range(steps):
+        got = swap(send, i)
+        if i + 1 == steps:
             break
         lanes = lanes // 2
         if lanes % 128:
@@ -315,25 +338,24 @@
     joined = call(
         functools.partial(readout_kernel, rows),
         S((owned, 2 * width), BF16),
-        (keep, got, frame),
+        (keep, got, held),
         flops=3 * rows * lanes,
     )
     far = far_by(joined)
     near = near_by(joined)
-    part, end_weight = call(
+    part = call(
         mid_conv_kernel,
-        (S((owned, out_width), F32), S((2, *decode_weight.shape[1:]), BF16)),
+        S((owned, out_width), F32),
         (joined, decode_weight),
         far=(1,),
-        scratch=(pltpu.VMEM(decode_weight.shape[1:], BF16), dma((3,))),
+        scratch=(pltpu.VMEM(taps_shape, BF16), dma((1,))),
         flops=2 * conv_flops,
-        grant=50,
     )
     objects = mask_weight.shape[1]
     logits = call(
-        last_kernel,
+        functools.partial(last_kernel, count),
         S((objects, owned), F32),
-        (odd, part, near, far, end_weight, mask_weight.T),
+        (part, near, far, end_weight, mask_weight.T),
         flops=4 * conv_flops,
     )
     return logits.T.reshape(query_value.shape[0], query_value.shape[1], objects)
@@ -344,7 +366,7 @@
     count = mesh.shape["mem"]
 
     def step(*args):
-        return shards(count, *args)
+        return shards(mesh.shape["groups"], count, *args)
 
     return jax.shard_map(
         step,

time: 46.4 us -> 43.9 us (0.946)
  the two profiles are of different devices: /device:TPU:25 before, /device:TPU:5 now
where the time goes in v1:
time: 43.9 us; the launch traced here: 43.2 us
  starting transfers between devices  17 us (39%)
  waiting for transfers between devices  16.6 us (38%)
  Pallas kernels  8.89 us (20%)
  between operations  0.73 us (2%)
    ppermute x6, waiting for transfers between devices, swap(): lax.ppermute(x, 'mem', [(i, i ^ order[i & 1][step]) for i in range(count)])  14.3 us
    pallas_call x11, Pallas kernels, call(): pl.pallas_call(kernel, out_shape=out, in_specs=[HB if i in far else SM if...  8.89 us
    ppermute x2, starting transfers between devices, near_by(): return lax.ppermute(x, 'mem', [(i, i ^ 1) for i in range(count)])  8.04 us
    ppermute x6, starting transfers between devices, swap(): lax.ppermute(x, 'mem', [(i, i ^ order[i & 1][step]) for i in range(count)])  7.74 us
    ppermute x1, waiting for transfers between devices, far_by(): return lax.ppermute(x, ('groups', 'mem'), links)  2.27 us
    ppermute x1, starting transfers between devices, far_by(): return lax.ppermute(x, ('groups', 'mem'), links)  1.19 us
  transfers between devices with their start and end apart: 9, of which 6 were waited for; matrix products, arithmetic and copies ran while one was open for 0% of the time, Pallas kernels for 11%

profile of v1, /device:TPU:5, one launch (start us, length us, event | category | flops | bytes accessed | tf_op | source)
XLA Modules:
  0.0 43.2 jit_solution(7220601084973545060)
XLA Ops:
  0.7 1.6 %shard_map.91 = (bf16[528,640]{1,0:T(8,128)(2,1)S(1)}, bf16[64,128]{1,0:T(8,128)(2,1)S(1)}) custom-call(bf16[512,128]{1,0:T(8,128)(2,1)} %bitcast.10, bf16[512,512]{1,0:T(8,128)(2,1)} %bitcast.9, s32[4,128]{1,0:T(4,128)} %lab_hbm.1, bf16[8,512]{1,0:T(8,128)(2,1)} %emb_hbm.1, bf16[64,128]{1,0:T(8,128)(2,1)} %bitcast.12, s32[1]{0:T(128)S(6)} %copy.10.count_ref), custom_call_target="tpu_custom_call" | custom-call | flops 4194304 | bytes 1374212 | tf_op jit(solution)/shard_map/pallas_call | solution.py:27
  2.3 0.7 %collective-permute-start = (bf16[528,640]{1,0:T(8,128)(2,1)S(1)}, bf16[528,640]{1,0:T(8,128)(2,1)S(1)}, u32[]{:S(2)}, u32[]{:S(2)}) collective-permute-start(bf16[528,640]{1,0:T(8,128)(2,1)S(1)} %get-tuple-element.13.mine_ref), channel_id=1, source_target_pairs={{0,1},{1,0},{2,3},{3,2},{4,5},{5,4},{6,7},{7,6},{8,9},{9,8},{10,11... | collective-permute-start | bytes 2027528 | tf_op jit(solution)/shard_map/ppermute | solution.py:256
  3.0 2.3 %collective-permute-start.1 = (bf16[64,128]{1,0:T(8,128)(2,1)}, bf16[64,128]{1,0:T(8,128)(2,1)S(1)}, u32[]{:S(2)}, u32[]{:S(2)}) collective-permute-start(bf16[64,128]{1,0:T(8,128)(2,1)} %bitcast.13), channel_id=1, source_target_pairs={{0,8},{1,9},{2,10},{3,11},{4,12},{5,13},{6,14},{7,15},{8,0},{9,1},... | collective-permute-start | bytes 49160 | tf_op jit(solution)/shard_map/ppermute | solution.py:253
  5.3 1.4 %collective-permute-done.1.b_ref = bf16[64,128]{1,0:T(8,128)(2,1)S(1)} collective-permute-done((bf16[64,128]{1,0:T(8,128)(2,1)}, bf16[64,128]{1,0:T(8,128)(2,1)S(1)}, u32[]{:S(2)}, u32[]{:S(2)}) %collective-permute-start.1) | collective-permute-done | bytes 16416 | tf_op jit(solution)/shard_map/ppermute | solution.py:253
  6.7 0.2 collective-permute-start.2
  6.9 2.6 %collective-permute-done.2.b_ref = bf16[128,128]{1,0:T(8,128)(2,1)S(1)} collective-permute-done((bf16[128,128]{1,0:T(8,128)(2,1)S(1)}, bf16[128,128]{1,0:T(8,128)(2,1)S(1)}, u32[]{:S(2)}, u32[]{:S(2)}) %collective-permute-start.2) | collective-permute-done | bytes 32800 | tf_op jit(solution)/shard_map/ppermute | solution.py:253
  9.5 1.3 %collective-permute-start.3 = (bf16[256,128]{1,0:T(8,128)(2,1)S(1)}, bf16[256,128]{1,0:T(8,128)(2,1)S(1)}, u32[]{:S(2)}, u32[]{:S(2)}) collective-permute-start(bf16[256,128]{1,0:T(8,128)(2,1)S(1)} %shard_map.93.q_ref), channel_id=1, source_target_pairs={{0,2},{1,5},{2,0},{3,7},{4,6},{5,1},{6,4},{7,3},{8,10},{9,13},{10,... | collective-permute-start | bytes 196616 | tf_op jit(solution)/shard_map/ppermute | solution.py:253
  10.8 1.8 %collective-permute-done.3.q_ref = bf16[256,128]{1,0:T(8,128)(2,1)S(1)} collective-permute-done((bf16[256,128]{1,0:T(8,128)(2,1)S(1)}, bf16[256,128]{1,0:T(8,128)(2,1)S(1)}, u32[]{:S(2)}, u32[]{:S(2)}) %collective-permute-start.3) | collective-permute-done | bytes 65568 | tf_op jit(solution)/shard_map/ppermute | solution.py:253
  12.6 0.0 collective-permute-done.other_ref
  12.6 0.9 %shard_map.95 = bf16[528,256]{1,0:T(8,128)(2,1)S(1)} custom-call(bf16[528,640]{1,0:T(8,128)(2,1)S(1)} %get-tuple-element.13.mine_ref, bf16[528,640]{1,0:T(8,128)(2,1)S(1)} %collective-permute-done.other_ref, bf16[256,128]{1,0:T(8,128)(2,1)S(1)} %collective-permute-done.3.q_ref), custom_call_target="tpu_custom_call" | custom-call | flops 335544320 | bytes 1687552 | tf_op jit(solution)/shard_map/pallas_call | solution.py:27
  13.5 1.4 %collective-permute-start.4 = (bf16[528,256]{1,0:T(8,128)(2,1)S(1)}, bf16[528,256]{1,0:T(8,128)(2,1)S(1)}, u32[]{:S(2)}, u32[]{:S(2)}) collective-permute-start(bf16[528,256]{1,0:T(8,128)(2,1)S(1)} %shard_map.95), channel_id=1, source_target_pairs={{0,2},{1,5},{2,0},{3,7},{4,6},{5,1},{6,4},{7,3},{8,10},{9,13},{10,... | collective-permute-start | bytes 811016 | tf_op jit(solution)/shard_map/ppermute | solution.py:253
  14.9 0.9 %shard_map.94.keep_ref = f32[528,256]{1,0:T(8,128)S(1)} custom-call(bf16[528,640]{1,0:T(8,128)(2,1)S(1)} %get-tuple-element.13.mine_ref, bf16[528,640]{1,0:T(8,128)(2,1)S(1)} %collective-permute-done.other_ref, bf16[256,128]{1,0:T(8,128)(2,1)S(1)} %shard_map.93.q_ref), custom_call_target="tpu_custom_call" | custom-call | flops 335544320 | bytes 1957888 | tf_op jit(solution)/shard_map/pallas_call | solution.py:27
  15.8 3.1 %collective-permute-done.4.got_ref = bf16[528,256]{1,0:T(8,128)(2,1)S(1)} collective-permute-done((bf16[528,256]{1,0:T(8,128)(2,1)S(1)}, bf16[528,256]{1,0:T(8,128)(2,1)S(1)}, u32[]{:S(2)}, u32[]{:S(2)}) %collective-permute-start.4) | collective-permute-done | bytes 270368 | tf_op jit(solution)/shard_map/ppermute | solution.py:253
  18.9 0.1 shard_map.96
  19.0 0.2 collective-permute-start.5
  19.2 5.4 %collective-permute-done.5.got_ref = bf16[528,128]{1,0:T(8,128)(2,1)S(1)} collective-permute-done((bf16[528,128]{1,0:T(8,128)(2,1)S(1)}, bf16[528,128]{1,0:T(8,128)(2,1)S(1)}, u32[]{:S(2)}, u32[]{:S(2)}) %collective-permute-start.5) | collective-permute-done | bytes 135200 | tf_op jit(solution)/shard_map/ppermute | solution.py:253
  24.6 0.1 shard_map.97
  24.7 2.4 %collective-permute-start.6 = (bf16[272,128]{1,0:T(8,128)(2,1)S(1)}, bf16[272,128]{1,0:T(8,128)(2,1)S(1)}, u32[]{:S(2)}, u32[]{:S(2)}) collective-permute-start(bf16[272,128]{1,0:T(8,128)(2,1)S(1)} %get-tuple-element.18), channel_id=1, source_target_pairs={{0,8},{1,9},{2,10},{3,11},{4,12},{5,13},{6,14},{7,15},{8,0},{9,1},... | collective-permute-start | bytes 208904 | tf_op jit(solution)/shard_map/ppermute | solution.py:253
  27.1 0.0 copy-start
  27.1 2.0 %shard_map.98 = (bf16[2,3,1024,256]{3,2,1,0:T(8,128)(2,1)S(1)}, bf16[64,512]{1,0:T(8,128)(2,1)S(1)}) custom-call(bf16[3,3,1024,256]{3,2,1,0:T(8,128)(2,1)} %w_hbm.3, bf16[64,512]{1,0:T(8,128)(2,1)} %bitcast.11), custom_call_target="tpu_custom_call" | custom-call | bytes 7995392 | tf_op jit(solution)/shard_map/pallas_call | solution.py:27
  29.0 0.0 collective-permute-done.6.got_ref
  29.1 0.1 shard_map.99.mid_ref
  29.2 7.3 %collective-permute-start.7 = (bf16[64,1024]{1,0:T(8,128)(2,1)S(1)}, bf16[64,1024]{1,0:T(8,128)(2,1)S(1)}, u32[]{:S(2)}, u32[]{:S(2)}) collective-permute-start(bf16[64,1024]{1,0:T(8,128)(2,1)S(1)} %shard_map.99.mid_ref), channel_id=1, source_target_pairs={{0,1},{1,0},{2,3},{3,2},{4,5},{5,4},{6,7},{7,6},{8,9},{9,8},{10,11... | collective-permute-start | bytes 393224 | tf_op jit(solution)/shard_map/ppermute | solution.py:256
  36.5 1.2 %collective-permute-start.8 = (bf16[64,1024]{1,0:T(8,128)(2,1)S(1)}, bf16[64,1024]{1,0:T(8,128)(2,1)S(1)}, u32[]{:S(2)}, u32[]{:S(2)}) collective-permute-start(bf16[64,1024]{1,0:T(8,128)(2,1)S(1)} %shard_map.99.mid_ref), channel_id=1, source_target_pairs={{1,2},{3,4},{5,6},{7,8},{9,10},{11,12},{13,14},{0,16},{15,31},{17,... | collective-permute-start | bytes 393224 | tf_op jit(solution)/shard_map/ppermute | solution.py:266
  37.7 1.8 %shard_map.100.sum_ref = f32[64,256]{1,0:T(8,128)S(1)} custom-call(bf16[64,1024]{1,0:T(8,128)(2,1)S(1)} %shard_map.99.mid_ref, bf16[3,3,1024,256]{3,2,1,0:T(8,128)(2,1)} %w_hbm.3), custom_call_target="tpu_custom_call" | custom-call | flops 100663296 | bytes 4915200 | tf_op jit(solution)/shard_map/pallas_call | solution.py:27
  39.5 0.0 collective-permute-done.7.near_ref
  39.5 2.3 %collective-permute-done.8.far_ref = bf16[64,1024]{1,0:T(8,128)(2,1)S(1)} collective-permute-done((bf16[64,1024]{1,0:T(8,128)(2,1)S(1)}, bf16[64,1024]{1,0:T(8,128)(2,1)S(1)}, u32[]{:S(2)}, u32[]{:S(2)}) %collective-permute-start.8) | collective-permute-done | bytes 131104 | tf_op jit(solution)/shard_map/ppermute | solution.py:266
  41.8 0.0 copy-done
  41.8 1.4 %shard_map.101 = f32[8,64]{1,0:T(8,128)} custom-call(f32[64,256]{1,0:T(8,128)S(1)} %shard_map.100.sum_ref, bf16[64,1024]{1,0:T(8,128)(2,1)S(1)} %collective-permute-done.7.near_ref, bf16[64,1024]{1,0:T(8,128)(2,1)S(1)} %collective-permute-done.8.far_ref, bf16[2,3,1024,256]{3,2,1,0:T(8,128)(2,1)S(1)} %get-tuple-element.20.w_ref, bf16[8,256]{1,0:T(8,128)(2,1)S(1)} %bitcast.8), custom_call_target="tpu_custom_call" | custom-call | flops 201326592 | bytes 3479552 | tf_op jit(solution)/shard_map/pallas_call | solution.py:27
  (2 shorter events, 0.0 us)
Async XLA Ops:
  2.3 10.3 %collective-permute-start = (bf16[528,640]{1,0:T(8,128)(2,1)S(1)}, bf16[528,640]{1,0:T(8,128)(2,1)S(1)}, u32[]{:S(2)}, u32[]{:S(2)}) collective-permute-start(bf16[528,640]{1,0:T(8,128)(2,1)S(1)} %get-tuple-element.13.mine_ref), channel_id=1, source_target_pairs={{0,1},{1,0},{2,3},{3,2},{4,5},{5,4},{6,7},{7,6},{8,9},{9,8},{10,11... | collective-permute-start | bytes 2027528 | tf_op jit(solution)/shard_map/ppermute | solution.py:256
  3.0 3.7 %collective-permute-start.1 = (bf16[64,128]{1,0:T(8,128)(2,1)}, bf16[64,128]{1,0:T(8,128)(2,1)S(1)}, u32[]{:S(2)}, u32[]{:S(2)}) collective-permute-start(bf16[64,128]{1,0:T(8,128)(2,1)} %bitcast.13), channel_id=1, source_target_pairs={{0,8},{1,9},{2,10},{3,11},{4,12},{5,13},{6,14},{7,15},{8,0},{9,1},... | collective-permute-start | bytes 49160 | tf_op jit(solution)/shard_map/ppermute | solution.py:253
  6.7 2.8 %collective-permute-start.2 = (bf16[128,128]{1,0:T(8,128)(2,1)S(1)}, bf16[128,128]{1,0:T(8,128)(2,1)S(1)}, u32[]{:S(2)}, u32[]{:S(2)}) collective-permute-start(bf16[128,128]{1,0:T(8,128)(2,1)S(1)} %shard_map.92.a_ref), channel_id=1, source_target_pairs={{0,4},{1,3},{2,6},{3,1},{4,0},{5,7},{6,2},{7,5},{8,12},{9,11},{10,... | collective-permute-start | bytes 98312 | tf_op jit(solution)/shard_map/ppermute | solution.py:253
  9.5 3.1 %collective-permute-start.3 = (bf16[256,128]{1,0:T(8,128)(2,1)S(1)}, bf16[256,128]{1,0:T(8,128)(2,1)S(1)}, u32[]{:S(2)}, u32[]{:S(2)}) collective-permute-start(bf16[256,128]{1,0:T(8,128)(2,1)S(1)} %shard_map.93.q_ref), channel_id=1, source_target_pairs={{0,2},{1,5},{2,0},{3,7},{4,6},{5,1},{6,4},{7,3},{8,10},{9,13},{10,... | collective-permute-start | bytes 196616 | tf_op jit(solution)/shard_map/ppermute | solution.py:253
  13.5 5.4 %collective-permute-start.4 = (bf16[528,256]{1,0:T(8,128)(2,1)S(1)}, bf16[528,256]{1,0:T(8,128)(2,1)S(1)}, u32[]{:S(2)}, u32[]{:S(2)}) collective-permute-start(bf16[528,256]{1,0:T(8,128)(2,1)S(1)} %shard_map.95), channel_id=1, source_target_pairs={{0,2},{1,5},{2,0},{3,7},{4,6},{5,1},{6,4},{7,3},{8,10},{9,13},{10,... | collective-permute-start | bytes 811016 | tf_op jit(solution)/shard_map/ppermute | solution.py:253
  19.0 5.6 %collective-permute-start.5 = (bf16[528,128]{1,0:T(8,128)(2,1)S(1)}, bf16[528,128]{1,0:T(8,128)(2,1)S(1)}, u32[]{:S(2)}, u32[]{:S(2)}) collective-permute-start(bf16[528,128]{1,0:T(8,128)(2,1)S(1)} %get-tuple-element.16), channel_id=1, source_target_pairs={{0,4},{1,3},{2,6},{3,1},{4,0},{5,7},{6,2},{7,5},{8,12},{9,11},{10,... | collective-permute-start | bytes 405512 | tf_op jit(solution)/shard_map/ppermute | solution.py:253
  24.7 4.4 %collective-permute-start.6 = (bf16[272,128]{1,0:T(8,128)(2,1)S(1)}, bf16[272,128]{1,0:T(8,128)(2,1)S(1)}, u32[]{:S(2)}, u32[]{:S(2)}) collective-permute-start(bf16[272,128]{1,0:T(8,128)(2,1)S(1)} %get-tuple-element.18), channel_id=1, source_target_pairs={{0,8},{1,9},{2,10},{3,11},{4,12},{5,13},{6,14},{7,15},{8,0},{9,1},... | collective-permute-start | bytes 208904 | tf_op jit(solution)/shard_map/ppermute | solution.py:253
  27.1 14.7 %copy-start = (bf16[256,8]{0,1:T(8,128)(2,1)S(1)}, bf16[256,8]{0,1:T(8,128)(2,1)}, u32[]{:S(2)}) copy-start(bf16[256,8]{0,1:T(8,128)(2,1)} %param.17) | copy-start | bytes 12292
  29.2 10.3 %collective-permute-start.7 = (bf16[64,1024]{1,0:T(8,128)(2,1)S(1)}, bf16[64,1024]{1,0:T(8,128)(2,1)S(1)}, u32[]{:S(2)}, u32[]{:S(2)}) collective-permute-start(bf16[64,1024]{1,0:T(8,128)(2,1)S(1)} %shard_map.99.mid_ref), channel_id=1, source_target_pairs={{0,1},{1,0},{2,3},{3,2},{4,5},{5,4},{6,7},{7,6},{8,9},{9,8},{10,11... | collective-permute-start | bytes 393224 | tf_op jit(solution)/shard_map/ppermute | solution.py:256
  36.5 5.3 %collective-permute-start.8 = (bf16[64,1024]{1,0:T(8,128)(2,1)S(1)}, bf16[64,1024]{1,0:T(8,128)(2,1)S(1)}, u32[]{:S(2)}, u32[]{:S(2)}) collective-permute-start(bf16[64,1024]{1,0:T(8,128)(2,1)S(1)} %shard_map.99.mid_ref), channel_id=1, source_target_pairs={{1,2},{3,4},{5,6},{7,8},{9,10},{11,12},{13,14},{0,16},{15,31},{17,... | collective-permute-start | bytes 393224 | tf_op jit(solution)/shard_map/ppermute | solution.py:266

commit v2 on v1

--- a/solution.py
+++ b/solution.py
@@ -150,13 +150,12 @@
     keep_out[rows : rows + PAD] = keep_tail(first(peak8)[0:1], first(mass8)[0:1])
 
 
-def readout_kernel(rows, keep_ref, got_ref, frame_ref, out_ref):
+def readout_kernel(rows, keep_ref, got_ref, out_ref):
     values, _, mass = merged(rows, keep_ref, got_ref)
     turned = (values / mass).T
     half = turned.shape[0] // 2
     out_ref[:, 0:rows] = turned[0:half].astype(BF16)
     out_ref[:, rows : 2 * rows] = turned[half:].astype(BF16)
-    out_ref[:, 2 * rows :] = frame_ref[...]
 
 
 def join_kernel(a_ref, b_ref, out_ref):
@@ -199,27 +198,38 @@
     return copies
 
 
-def stage_kernel(w_hbm, frame_hbm, ends_ref, frame_ref, sems):
-    pairs = (
-        (frame_hbm, frame_ref),
-        (w_hbm.at[0], ends_ref.at[0]),
-        (w_hbm.at[2], ends_ref.at[1]),
-    )
+def stage_kernel(w_hbm, ends_ref, sems):
+    low = pl.ds(0, ends_ref.shape[2])
+    pairs = [(w_hbm.at[2 * i, :, low], ends_ref.at[i]) for i in range(2)]
     for copy in copy_all(pairs, sems):
         copy.wait()
 
 
+def frame_conv_kernel(count, near_ref, far_ref, frame_hbm, w_hbm, out_ref, frame_ref, w_ref, sems):
+    width = frame_ref.shape[1]
+    pairs = [(frame_hbm, frame_ref)]
+    pairs += [(w_hbm.at[i, :, pl.ds(width, width)], w_ref.at[i]) for i in range(3)]
+    for copy in copy_all(pairs, sems):
+        copy.wait()
+    up, down = ends(count, near_ref, far_ref)
+    lines = (up, frame_ref[...], down)
+    out_ref[...] = taps([(line, functools.partial(column, w_ref, i)) for i, line in enumerate(lines)])
+
+
+def column(w_ref, row, col):
+    return w_ref[row, col]
+
+
 def mid_conv_kernel(mid_ref, w_hbm, out_ref, w_ref, sems):
-    for copy in copy_all(((w_hbm.at[1], w_ref),), sems):
+    for copy in copy_all([(w_hbm.at[1, :, pl.ds(0, w_ref.shape[1])], w_ref)], sems):
         copy.wait()
-    out_ref[...] = taps(((mid_ref[...], lambda col: w_ref[col]),))
-
-
-def last_kernel(count, sum_ref, near_ref, far_ref, w_ref, mask_ref, out_ref):
-    up, down = ends(count, near_ref, far_ref)
-    total = sum_ref[...] + taps(
-        ((up, lambda col: w_ref[0, col]), (down, lambda col: w_ref[1, col]))
-    )
+    out_ref[...] = taps([(mid_ref[...], lambda col: w_ref[col])])
+
+
+def last_kernel(count, frame_sum_ref, mid_sum_ref, near_ref, far_ref, w_ref, mask_ref, out_ref):
+    lines = ends(count, near_ref, far_ref)
+    total = taps([(line, functools.partial(column, w_ref, i)) for i, line in enumerate(lines)])
+    total = total + mid_sum_ref[...] + frame_sum_ref[...]
     hidden = jnp.maximum(total, 0.0).astype(BF16)
     out_ref[...] = lax.dot_general(
         mask_ref[...], hidden, (((1,), (1,)), ((), ())), preferred_element_type=F32
@@ -246,11 +256,11 @@
     out_width = decode_weight.shape[3]
 
     steps = count.bit_length() - 2
-    order = [[1 << i for i in range(1, steps + 1)] for _ in range(2)]
-    order[1][0:2] = order[1][1::-1]
+    order = [(1 << i) + 1 for i in range(1, steps + 1)]
+    order[0:2] = order[1::-1]
 
     def swap(x, step):
-        return lax.ppermute(x, "mem", [(i, i ^ order[i & 1][step]) for i in range(count)])
+        return lax.ppermute(x, "mem", [(i, i ^ order[step]) for i in range(count)])
 
     def near_by(x):
         return lax.ppermute(x, "mem", [(i, i ^ 1) for i in range(count)])
@@ -310,13 +320,24 @@
     keep = attend_call(queries, False, F32)
     send = attend_call(theirs, True, BF16)
     conv_flops = 2 * owned * width * out_width * 3
-    taps_shape = decode_weight.shape[1:]
-    end_weight, held = call(
+    columns = decode_weight.shape[1]
+    half_taps = (columns, width, out_width)
+    end_weight = call(
         stage_kernel,
-        (S((2, *taps_shape), BF16), S(frame.shape, BF16)),
-        (decode_weight, frame),
-        far=(0, 1),
-        scratch=(dma((3,)),),
+        S((2, *half_taps), BF16),
+        (decode_weight,),
+        far=(0,),
+        scratch=(dma((2,)),),
+    )
+    frame_far = far_by(frame)
+    frame_near = near_by(frame)
+    frame_part = call(
+        functools.partial(frame_conv_kernel, count),
+        S((owned, out_width), F32),
+        (frame_near, frame_far, frame, decode_weight),
+        far=(2, 3),
+        scratch=(pltpu.VMEM(frame.shape, BF16), pltpu.VMEM((3, *half_taps), BF16), dma((4,))),
+        flops=3 * conv_flops,
     )
     rows = width
     for i in range(steps):
@@ -335,28 +356,28 @@
             flops=3 * rows * lanes,
         )
         rows = out_rows - PAD
-    joined = call(
+    readout = call(
         functools.partial(readout_kernel, rows),
-        S((owned, 2 * width), BF16),
-        (keep, got, held),
+        S((owned, width), BF16),
+        (keep, got),
         flops=3 * rows * lanes,
     )
-    far = far_by(joined)
-    near = near_by(joined)
-    part = call(
+    far = far_by(readout)
+    near = near_by(readout)
+    mid_part = call(
         mid_conv_kernel,
         S((owned, out_width), F32),
-        (joined, decode_weight),
+        (readout, decode_weight),
         far=(1,),
-        scratch=(pltpu.VMEM(taps_shape, BF16), dma((1,))),
-        flops=2 * conv_flops,
+        scratch=(pltpu.VMEM(half_taps, BF16), dma((1,))),
+        flops=conv_flops,
     )
     objects = mask_weight.shape[1]
     logits = call(
         functools.partial(last_kernel, count),
         S((objects, owned), F32),
-        (part, near, far, end_weight, mask_weight.T),
-        flops=4 * conv_flops,
+        (frame_part, mid_part, near, far, end_weight, mask_weight.T),
+        flops=2 * conv_flops,
     )
     return logits.T.reshape(query_value.shape[0], query_value.shape[1], objects)
 

time: 43.9 us -> 44.7 us (1.018)
  the two profiles are of different devices: /device:TPU:5 before, /device:TPU:0 now
where the time goes in v2:
time: 44.7 us; the launch traced here: 44.5 us
  waiting for transfers between devices  20.8 us (47%)
  starting transfers between devices  13 us (29%)
  Pallas kernels  9.86 us (22%)
  between operations  0.82 us (2%)
    ppermute x6, waiting for transfers between devices, swap(): return lax.ppermute(x, 'mem', [(i, i ^ order[step]) for i in range(count)])  20.8 us
    ppermute x6, starting transfers between devices, swap(): return lax.ppermute(x, 'mem', [(i, i ^ order[step]) for i in range(count)])  10.6 us
    pallas_call x12, Pallas kernels, call(): pl.pallas_call(kernel, out_shape=out, in_specs=[HB if i in far else SM if...  9.86 us
    ppermute x2, starting transfers between devices, far_by(): return lax.ppermute(x, ('groups', 'mem'), links)  1.6 us
  transfers between devices with their start and end apart: 11, of which 6 were waited for; matrix products, arithmetic and copies ran while one was open for 0% of the time, Pallas kernels for 14%

profile of v2, /device:TPU:0, one launch (start us, length us, event | category | flops | bytes accessed | tf_op | source)
XLA Modules:
  0.0 44.5 jit_solution(1425986420171176961)
XLA Ops:
  0.0 0.0 copy-start.1
  0.7 1.6 %shard_map.92 = (bf16[528,640]{1,0:T(8,128)(2,1)S(1)}, bf16[64,128]{1,0:T(8,128)(2,1)S(1)}) custom-call(bf16[512,128]{1,0:T(8,128)(2,1)} %bitcast.10, bf16[512,512]{1,0:T(8,128)(2,1)} %bitcast.9, s32[4,128]{1,0:T(4,128)} %lab_hbm.1, bf16[8,512]{1,0:T(8,128)(2,1)} %emb_hbm.1, bf16[64,128]{1,0:T(8,128)(2,1)} %bitcast.14, s32[1]{0:T(128)S(6)} %copy.10.count_ref), custom_call_target="tpu_custom_call" | custom-call | flops 4194304 | bytes 1374212 | tf_op jit(solution)/shard_map/pallas_call | solution.py:27
  2.3 0.6 %collective-permute-start.2 = (bf16[528,640]{1,0:T(8,128)(2,1)S(1)}, bf16[528,640]{1,0:T(8,128)(2,1)S(1)}, u32[]{:S(2)}, u32[]{:S(2)}) collective-permute-start(bf16[528,640]{1,0:T(8,128)(2,1)S(1)} %get-tuple-element.11.mine_ref), channel_id=1, source_target_pairs={{0,1},{1,0},{2,3},{3,2},{4,5},{5,4},{6,7},{7,6},{8,9},{9,8},{10,11... | collective-permute-start | bytes 2027528 | tf_op jit(solution)/shard_map/ppermute | solution.py:266
  2.8 3.7 %collective-permute-start.3 = (bf16[64,128]{1,0:T(8,128)(2,1)}, bf16[64,128]{1,0:T(8,128)(2,1)S(1)}, u32[]{:S(2)}, u32[]{:S(2)}) collective-permute-start(bf16[64,128]{1,0:T(8,128)(2,1)} %bitcast.15), channel_id=1, source_target_pairs={{0,9},{1,8},{2,11},{3,10},{4,13},{5,12},{6,15},{7,14},{8,1},{9,0},... | collective-permute-start | bytes 49160 | tf_op jit(solution)/shard_map/ppermute | solution.py:263
  6.5 1.7 %collective-permute-done.3.b_ref = bf16[64,128]{1,0:T(8,128)(2,1)S(1)} collective-permute-done((bf16[64,128]{1,0:T(8,128)(2,1)}, bf16[64,128]{1,0:T(8,128)(2,1)S(1)}, u32[]{:S(2)}, u32[]{:S(2)}) %collective-permute-start.3) | collective-permute-done | bytes 16416 | tf_op jit(solution)/shard_map/ppermute | solution.py:263
  8.2 1.5 %collective-permute-start.4 = (bf16[128,128]{1,0:T(8,128)(2,1)S(1)}, bf16[128,128]{1,0:T(8,128)(2,1)S(1)}, u32[]{:S(2)}, u32[]{:S(2)}) collective-permute-start(bf16[128,128]{1,0:T(8,128)(2,1)S(1)} %shard_map.93.a_ref), channel_id=1, source_target_pairs={{0,3},{1,2},{2,1},{3,0},{4,7},{5,6},{6,5},{7,4},{8,11},{9,10},{10,... | collective-permute-start | bytes 98312 | tf_op jit(solution)/shard_map/ppermute | solution.py:263
  9.7 1.9 %collective-permute-done.4.b_ref = bf16[128,128]{1,0:T(8,128)(2,1)S(1)} collective-permute-done((bf16[128,128]{1,0:T(8,128)(2,1)S(1)}, bf16[128,128]{1,0:T(8,128)(2,1)S(1)}, u32[]{:S(2)}, u32[]{:S(2)}) %collective-permute-start.4) | collective-permute-done | bytes 32800 | tf_op jit(solution)/shard_map/ppermute | solution.py:263
  11.6 1.5 %collective-permute-start.5 = (bf16[256,128]{1,0:T(8,128)(2,1)S(1)}, bf16[256,128]{1,0:T(8,128)(2,1)S(1)}, u32[]{:S(2)}, u32[]{:S(2)}) collective-permute-start(bf16[256,128]{1,0:T(8,128)(2,1)S(1)} %shard_map.94.q_ref), channel_id=1, source_target_pairs={{0,5},{1,4},{2,7},{3,6},{4,1},{5,0},{6,3},{7,2},{8,13},{9,12},{10,... | collective-permute-start | bytes 196616 | tf_op jit(solution)/shard_map/ppermute | solution.py:263
  13.1 2.6 %collective-permute-done.5.q_ref = bf16[256,128]{1,0:T(8,128)(2,1)S(1)} collective-permute-done((bf16[256,128]{1,0:T(8,128)(2,1)S(1)}, bf16[256,128]{1,0:T(8,128)(2,1)S(1)}, u32[]{:S(2)}, u32[]{:S(2)}) %collective-permute-start.5) | collective-permute-done | bytes 65568 | tf_op jit(solution)/shard_map/ppermute | solution.py:263
  15.7 0.0 collective-permute-done.2.other_ref
  15.7 0.9 %shard_map.96 = bf16[528,256]{1,0:T(8,128)(2,1)S(1)} custom-call(bf16[528,640]{1,0:T(8,128)(2,1)S(1)} %get-tuple-element.11.mine_ref, bf16[528,640]{1,0:T(8,128)(2,1)S(1)} %collective-permute-done.2.other_ref, bf16[256,128]{1,0:T(8,128)(2,1)S(1)} %collective-permute-done.5.q_ref), custom_call_target="tpu_custom_call" | custom-call | flops 335544320 | bytes 1687552 | tf_op jit(solution)/shard_map/pallas_call | solution.py:27
  16.6 1.3 %collective-permute-start.6 = (bf16[528,256]{1,0:T(8,128)(2,1)S(1)}, bf16[528,256]{1,0:T(8,128)(2,1)S(1)}, u32[]{:S(2)}, u32[]{:S(2)}) collective-permute-start(bf16[528,256]{1,0:T(8,128)(2,1)S(1)} %shard_map.96), channel_id=1, source_target_pairs={{0,5},{1,4},{2,7},{3,6},{4,1},{5,0},{6,3},{7,2},{8,13},{9,12},{10,... | collective-permute-start | bytes 811016 | tf_op jit(solution)/shard_map/ppermute | solution.py:263
  17.9 0.9 %shard_map.95.keep_ref = f32[528,256]{1,0:T(8,128)S(1)} custom-call(bf16[528,640]{1,0:T(8,128)(2,1)S(1)} %get-tuple-element.11.mine_ref, bf16[528,640]{1,0:T(8,128)(2,1)S(1)} %collective-permute-done.2.other_ref, bf16[256,128]{1,0:T(8,128)(2,1)S(1)} %shard_map.94.q_ref), custom_call_target="tpu_custom_call" | custom-call | flops 335544320 | bytes 1957888 | tf_op jit(solution)/shard_map/pallas_call | solution.py:27
  18.8 6.4 %collective-permute-done.6.got_ref = bf16[528,256]{1,0:T(8,128)(2,1)S(1)} collective-permute-done((bf16[528,256]{1,0:T(8,128)(2,1)S(1)}, bf16[528,256]{1,0:T(8,128)(2,1)S(1)}, u32[]{:S(2)}, u32[]{:S(2)}) %collective-permute-start.6) | collective-permute-done | bytes 270368 | tf_op jit(solution)/shard_map/ppermute | solution.py:263
  25.2 0.1 shard_map.97
  25.3 0.9 %collective-permute-start.7 = (bf16[528,128]{1,0:T(8,128)(2,1)S(1)}, bf16[528,128]{1,0:T(8,128)(2,1)S(1)}, u32[]{:S(2)}, u32[]{:S(2)}) collective-permute-start(bf16[528,128]{1,0:T(8,128)(2,1)S(1)} %get-tuple-element.14), channel_id=1, source_target_pairs={{0,3},{1,2},{2,1},{3,0},{4,7},{5,6},{6,5},{7,4},{8,11},{9,10},{10,... | collective-permute-start | bytes 405512 | tf_op jit(solution)/shard_map/ppermute | solution.py:263
  26.2 4.7 %collective-permute-done.7.got_ref = bf16[528,128]{1,0:T(8,128)(2,1)S(1)} collective-permute-done((bf16[528,128]{1,0:T(8,128)(2,1)S(1)}, bf16[528,128]{1,0:T(8,128)(2,1)S(1)}, u32[]{:S(2)}, u32[]{:S(2)}) %collective-permute-start.7) | collective-permute-done | bytes 135200 | tf_op jit(solution)/shard_map/ppermute | solution.py:263
  30.9 0.1 shard_map.98
  31.1 1.7 %collective-permute-start.8 = (bf16[272,128]{1,0:T(8,128)(2,1)S(1)}, bf16[272,128]{1,0:T(8,128)(2,1)S(1)}, u32[]{:S(2)}, u32[]{:S(2)}) collective-permute-start(bf16[272,128]{1,0:T(8,128)(2,1)S(1)} %get-tuple-element.16), channel_id=1, source_target_pairs={{0,9},{1,8},{2,11},{3,10},{4,13},{5,12},{6,15},{7,14},{8,1},{9,0},... | collective-permute-start | bytes 208904 | tf_op jit(solution)/shard_map/ppermute | solution.py:263
  32.7 0.0 copy-done.1
  32.7 0.1 collective-permute-start
  32.8 1.5 %collective-permute-start.1 = (bf16[64,512]{1,0:T(8,128)(2,1)S(1)}, bf16[64,512]{1,0:T(8,128)(2,1)S(1)}, u32[]{:S(2)}, u32[]{:S(2)}) collective-permute-start(bf16[64,512]{1,0:T(8,128)(2,1)S(1)} %bitcast.13), channel_id=1, source_target_pairs={{1,2},{3,4},{5,6},{7,8},{9,10},{11,12},{13,14},{0,16},{15,31},{17,... | collective-permute-start | bytes 196616 | tf_op jit(solution)/shard_map/ppermute | solution.py:276
  34.3 3.6 %collective-permute-done.8.got_ref = bf16[272,128]{1,0:T(8,128)(2,1)S(1)} collective-permute-done((bf16[272,128]{1,0:T(8,128)(2,1)S(1)}, bf16[272,128]{1,0:T(8,128)(2,1)S(1)}, u32[]{:S(2)}, u32[]{:S(2)}) %collective-permute-start.8) | collective-permute-done | bytes 69664 | tf_op jit(solution)/shard_map/ppermute | solution.py:263
  37.9 0.1 shard_map.99.mid_ref
  38.0 0.1 collective-permute-start.10
  38.1 0.1 collective-permute-start.9
  38.2 1.4 %shard_map.101.w_ref = bf16[2,3,512,256]{3,2,1,0:T(8,128)(2,1)S(1)} custom-call(bf16[3,3,1024,256]{3,2,1,0:T(8,128)(2,1)} %w_hbm.5), custom_call_target="tpu_custom_call" | custom-call | bytes 6291456 | tf_op jit(solution)/shard_map/pallas_call | solution.py:27
  39.6 0.0 copy-start
  39.7 0.0 collective-permute-done.near_ref
  39.7 0.0 collective-permute-done.1.far_ref
  39.7 2.2 %shard_map.91.frame_sum_ref = f32[64,256]{1,0:T(8,128)S(1)} custom-call(bf16[64,512]{1,0:T(8,128)(2,1)S(1)} %collective-permute-done.near_ref, bf16[64,512]{1,0:T(8,128)(2,1)S(1)} %collective-permute-done.1.far_ref, bf16[64,512]{1,0:T(8,128)(2,1)} %bitcast.11, bf16[3,3,1024,256]{3,2,1,0:T(8,128)(2,1)} %w_hbm.5), custom_call_target="tpu_custom_call" | custom-call | flops 150994944 | bytes 4980736 | tf_op jit(solution)/shard_map/pallas_call | solution.py:27
  41.9 1.4 %shard_map.100.mid_sum_ref = f32[64,256]{1,0:T(8,128)S(1)} custom-call(bf16[64,512]{1,0:T(8,128)(2,1)S(1)} %shard_map.99.mid_ref, bf16[3,3,1024,256]{3,2,1,0:T(8,128)(2,1)} %w_hbm.5), custom_call_target="tpu_custom_call" | custom-call | flops 50331648 | bytes 4849664 | tf_op jit(solution)/shard_map/pallas_call | solution.py:27
  43.3 0.0 collective-permute-done.10.far_ref
  43.3 0.0 collective-permute-done.9.near_ref
  43.3 0.0 copy-done
  43.4 1.1 %shard_map.102 = f32[8,64]{1,0:T(8,128)} custom-call(f32[64,256]{1,0:T(8,128)S(1)} %shard_map.91.frame_sum_ref, f32[64,256]{1,0:T(8,128)S(1)} %shard_map.100.mid_sum_ref, bf16[64,512]{1,0:T(8,128)(2,1)S(1)} %collective-permute-done.9.near_ref, bf16[64,512]{1,0:T(8,128)(2,1)S(1)} %collective-permute-done.10.far_ref, ...), custom_call_target="tpu_custom_call" | custom-call | flops 100663296 | bytes 1841152 | tf_op jit(solution)/shard_map/pallas_call | solution.py:27
  (2 shorter events, 0.0 us)
Async XLA Ops:
  0.0 32.7 %copy-start.1 = (bf16[1,64,512]{2,1,0:T(8,128)(2,1)S(1)}, bf16[1,64,512]{2,1,0:T(8,128)(2,1)}, u32[]{:S(2)}) copy-start(bf16[1,64,512]{2,1,0:T(8,128)(2,1)} %param.14) | copy-start | bytes 196612
  2.3 13.4 %collective-permute-start.2 = (bf16[528,640]{1,0:T(8,128)(2,1)S(1)}, bf16[528,640]{1,0:T(8,128)(2,1)S(1)}, u32[]{:S(2)}, u32[]{:S(2)}) collective-permute-start(bf16[528,640]{1,0:T(8,128)(2,1)S(1)} %get-tuple-element.11.mine_ref), channel_id=1, source_target_pairs={{0,1},{1,0},{2,3},{3,2},{4,5},{5,4},{6,7},{7,6},{8,9},{9,8},{10,11... | collective-permute-start | bytes 2027528 | tf_op jit(solution)/shard_map/ppermute | solution.py:266
  2.8 5.3 %collective-permute-start.3 = (bf16[64,128]{1,0:T(8,128)(2,1)}, bf16[64,128]{1,0:T(8,128)(2,1)S(1)}, u32[]{:S(2)}, u32[]{:S(2)}) collective-permute-start(bf16[64,128]{1,0:T(8,128)(2,1)} %bitcast.15), channel_id=1, source_target_pairs={{0,9},{1,8},{2,11},{3,10},{4,13},{5,12},{6,15},{7,14},{8,1},{9,0},... | collective-permute-start | bytes 49160 | tf_op jit(solution)/shard_map/ppermute | solution.py:263
  8.2 3.4 %collective-permute-start.4 = (bf16[128,128]{1,0:T(8,128)(2,1)S(1)}, bf16[128,128]{1,0:T(8,128)(2,1)S(1)}, u32[]{:S(2)}, u32[]{:S(2)}) collective-permute-start(bf16[128,128]{1,0:T(8,128)(2,1)S(1)} %shard_map.93.a_ref), channel_id=1, source_target_pairs={{0,3},{1,2},{2,1},{3,0},{4,7},{5,6},{6,5},{7,4},{8,11},{9,10},{10,... | collective-permute-start | bytes 98312 | tf_op jit(solution)/shard_map/ppermute | solution.py:263
  11.6 4.1 %collective-permute-start.5 = (bf16[256,128]{1,0:T(8,128)(2,1)S(1)}, bf16[256,128]{1,0:T(8,128)(2,1)S(1)}, u32[]{:S(2)}, u32[]{:S(2)}) collective-permute-start(bf16[256,128]{1,0:T(8,128)(2,1)S(1)} %shard_map.94.q_ref), channel_id=1, source_target_pairs={{0,5},{1,4},{2,7},{3,6},{4,1},{5,0},{6,3},{7,2},{8,13},{9,12},{10,... | collective-permute-start | bytes 196616 | tf_op jit(solution)/shard_map/ppermute | solution.py:263
  16.6 8.6 %collective-permute-start.6 = (bf16[528,256]{1,0:T(8,128)(2,1)S(1)}, bf16[528,256]{1,0:T(8,128)(2,1)S(1)}, u32[]{:S(2)}, u32[]{:S(2)}) collective-permute-start(bf16[528,256]{1,0:T(8,128)(2,1)S(1)} %shard_map.96), channel_id=1, source_target_pairs={{0,5},{1,4},{2,7},{3,6},{4,1},{5,0},{6,3},{7,2},{8,13},{9,12},{10,... | collective-permute-start | bytes 811016 | tf_op jit(solution)/shard_map/ppermute | solution.py:263
  25.3 5.6 %collective-permute-start.7 = (bf16[528,128]{1,0:T(8,128)(2,1)S(1)}, bf16[528,128]{1,0:T(8,128)(2,1)S(1)}, u32[]{:S(2)}, u32[]{:S(2)}) collective-permute-start(bf16[528,128]{1,0:T(8,128)(2,1)S(1)} %get-tuple-element.14), channel_id=1, source_target_pairs={{0,3},{1,2},{2,1},{3,0},{4,7},{5,6},{6,5},{7,4},{8,11},{9,10},{10,... | collective-permute-start | bytes 405512 | tf_op jit(solution)/shard_map/ppermute | solution.py:263
  31.1 6.9 %collective-permute-start.8 = (bf16[272,128]{1,0:T(8,128)(2,1)S(1)}, bf16[272,128]{1,0:T(8,128)(2,1)S(1)}, u32[]{:S(2)}, u32[]{:S(2)}) collective-permute-start(bf16[272,128]{1,0:T(8,128)(2,1)S(1)} %get-tuple-element.16), channel_id=1, source_target_pairs={{0,9},{1,8},{2,11},{3,10},{4,13},{5,12},{6,15},{7,14},{8,1},{9,0},... | collective-permute-start | bytes 208904 | tf_op jit(solution)/shard_map/ppermute | solution.py:263
  32.7 6.9 %collective-permute-start = (bf16[64,512]{1,0:T(8,128)(2,1)S(1)}, bf16[64,512]{1,0:T(8,128)(2,1)S(1)}, u32[]{:S(2)}, u32[]{:S(2)}) collective-permute-start(bf16[64,512]{1,0:T(8,128)(2,1)S(1)} %bitcast.12), channel_id=1, source_target_pairs={{0,1},{1,0},{2,3},{3,2},{4,5},{5,4},{6,7},{7,6},{8,9},{9,8},{10,11... | collective-permute-start | bytes 196616 | tf_op jit(solution)/shard_map/ppermute | solution.py:266
  32.8 6.9 %collective-permute-start.1 = (bf16[64,512]{1,0:T(8,128)(2,1)S(1)}, bf16[64,512]{1,0:T(8,128)(2,1)S(1)}, u32[]{:S(2)}, u32[]{:S(2)}) collective-permute-start(bf16[64,512]{1,0:T(8,128)(2,1)S(1)} %bitcast.13), channel_id=1, source_target_pairs={{1,2},{3,4},{5,6},{7,8},{9,10},{11,12},{13,14},{0,16},{15,31},{17,... | collective-permute-start | bytes 196616 | tf_op jit(solution)/shard_map/ppermute | solution.py:276
  38.0 5.3 %collective-permute-start.10 = (bf16[64,512]{1,0:T(8,128)(2,1)S(1)}, bf16[64,512]{1,0:T(8,128)(2,1)S(1)}, u32[]{:S(2)}, u32[]{:S(2)}) collective-permute-start(bf16[64,512]{1,0:T(8,128)(2,1)S(1)} %shard_map.99.mid_ref), channel_id=1, source_target_pairs={{1,2},{3,4},{5,6},{7,8},{9,10},{11,12},{13,14},{0,16},{15,31},{17,... | collective-permute-start | bytes 196616 | tf_op jit(solution)/shard_map/ppermute | solution.py:276
  38.1 5.2 %collective-permute-start.9 = (bf16[64,512]{1,0:T(8,128)(2,1)S(1)}, bf16[64,512]{1,0:T(8,128)(2,1)S(1)}, u32[]{:S(2)}, u32[]{:S(2)}) collective-permute-start(bf16[64,512]{1,0:T(8,128)(2,1)S(1)} %shard_map.99.mid_ref), channel_id=1, source_target_pairs={{0,1},{1,0},{2,3},{3,2},{4,5},{5,4},{6,7},{7,6},{8,9},{9,8},{10,11... | collective-permute-start | bytes 196616 | tf_op jit(solution)/shard_map/ppermute | solution.py:266
  39.6 3.7 %copy-start = (bf16[256,8]{0,1:T(8,128)(2,1)S(1)}, bf16[256,8]{0,1:T(8,128)(2,1)}, u32[]{:S(2)}) copy-start(bf16[256,8]{0,1:T(8,128)(2,1)} %param.17) | copy-start | bytes 12292

commit v3 on v1

--- a/solution.py
+++ b/solution.py
@@ -150,13 +150,23 @@
     keep_out[rows : rows + PAD] = keep_tail(first(peak8)[0:1], first(mass8)[0:1])
 
 
-def readout_kernel(rows, keep_ref, got_ref, frame_ref, out_ref):
+def far_row():
+    return 2 - 2 * lax.rem(lax.axis_index("mem"), 2)
+
+
+def readout_kernel(rows, keep_ref, got_ref, frame_ref, w_ref, out_ref, far_ref):
     values, _, mass = merged(rows, keep_ref, got_ref)
     turned = (values / mass).T
     half = turned.shape[0] // 2
-    out_ref[:, 0:rows] = turned[0:half].astype(BF16)
-    out_ref[:, rows : 2 * rows] = turned[half:].astype(BF16)
-    out_ref[:, 2 * rows :] = frame_ref[...]
+    line = jnp.concatenate([turned[0:half], turned[half:]], axis=1).astype(BF16)
+    out_ref[...] = line
+    far_ref[...] = frame_ref[...] + taps(line, w_ref)
+
+
+def rest_kernel(line_ref, frame_ref, w_ref, near_ref, mid_ref):
+    line = line_ref[...]
+    near_ref[...] = frame_ref[0] + taps(line, w_ref.at[0])
+    mid_ref[...] = frame_ref[1] + taps(line, w_ref.at[1])
 
 
 def join_kernel(a_ref, b_ref, out_ref):
@@ -173,23 +183,11 @@
     return left + right
 
 
-def taps(lines):
-    total = []
-    for col in range(3):
-        acc = None
-        for line, weight in lines:
-            term = jnp.dot(line, weight(col), preferred_element_type=F32)
-            acc = term if acc is None else acc + term
-        total.append(acc)
-    return slide(total[0], total[2]) + total[1]
-
-
-def ends(count, near_ref, far_ref):
-    place = lax.axis_index("mem")
-    odd = lax.rem(place, 2) == 1
-    near, far = near_ref[...], far_ref[...]
-    far = jnp.where((place == 0) | (place == count - 1), jnp.zeros_like(far), far)
-    return jnp.where(odd, near, far), jnp.where(odd, far, near)
+def taps(line, w_ref):
+    left, mid, right = (
+        jnp.dot(line, w_ref[col], preferred_element_type=F32) for col in range(3)
+    )
+    return slide(left, right) + mid
 
 
 def copy_all(pairs, sems):
@@ -199,28 +197,39 @@
     return copies
 
 
-def stage_kernel(w_hbm, frame_hbm, ends_ref, frame_ref, sems):
-    pairs = (
-        (frame_hbm, frame_ref),
-        (w_hbm.at[0], ends_ref.at[0]),
-        (w_hbm.at[2], ends_ref.at[1]),
-    )
-    for copy in copy_all(pairs, sems):
+def weight_copies(w_hbm, channels, far_ref, rest_ref):
+    far = far_row()
+    return [
+        (w_hbm.at[far, :, channels], far_ref),
+        (w_hbm.at[2 - far, :, channels], rest_ref.at[0]),
+        (w_hbm.at[1, :, channels], rest_ref.at[1]),
+    ]
+
+
+def frame_kernel(frame_hbm, w_hbm, far_ref, rest_ref, frame_ref, wfar_ref, wrest_ref, sems):
+    width = frame_ref.shape[1]
+    pairs = weight_copies(w_hbm, pl.ds(width, width), wfar_ref, wrest_ref)
+    copies = copy_all([(frame_hbm, frame_ref)] + pairs, sems)
+    copies[0].wait()
+    copies[1].wait()
+    line = frame_ref[...]
+    far_ref[...] = taps(line, wfar_ref)
+    for i in range(2):
+        copies[2 + i].wait()
+        rest_ref[i] = taps(line, wrest_ref.at[i])
+
+
+def stage_kernel(w_hbm, far_ref, rest_ref, sems):
+    low = pl.ds(0, far_ref.shape[1])
+    for copy in copy_all(weight_copies(w_hbm, low, far_ref, rest_ref), sems):
         copy.wait()
 
 
-def mid_conv_kernel(mid_ref, w_hbm, out_ref, w_ref, sems):
-    for copy in copy_all(((w_hbm.at[1], w_ref),), sems):
-        copy.wait()
-    out_ref[...] = taps(((mid_ref[...], lambda col: w_ref[col]),))
-
-
-def last_kernel(count, sum_ref, near_ref, far_ref, w_ref, mask_ref, out_ref):
-    up, down = ends(count, near_ref, far_ref)
-    total = sum_ref[...] + taps(
-        ((up, lambda col: w_ref[0, col]), (down, lambda col: w_ref[1, col]))
-    )
-    hidden = jnp.maximum(total, 0.0).astype(BF16)
+def last_kernel(count, mid_ref, near_ref, far_ref, mask_ref, out_ref):
+    place = lax.axis_index("mem")
+    far = far_ref[...]
+    far = jnp.where((place == 0) | (place == count - 1), jnp.zeros_like(far), far)
+    hidden = jnp.maximum(mid_ref[...] + near_ref[...] + far, 0.0).astype(BF16)
     out_ref[...] = lax.dot_general(
         mask_ref[...], hidden, (((1,), (1,)), ((), ())), preferred_element_type=F32
     )
@@ -246,11 +255,11 @@
     out_width = decode_weight.shape[3]
 
     steps = count.bit_length() - 2
-    order = [[1 << i for i in range(1, steps + 1)] for _ in range(2)]
-    order[1][0:2] = order[1][1::-1]
+    order = [1 << i for i in range(1, steps + 1)]
+    order[0:2] = order[1::-1]
 
     def swap(x, step):
-        return lax.ppermute(x, "mem", [(i, i ^ order[i & 1][step]) for i in range(count)])
+        return lax.ppermute(x, "mem", [(i, i ^ order[step]) for i in range(count)])
 
     def near_by(x):
         return lax.ppermute(x, "mem", [(i, i ^ 1) for i in range(count)])
@@ -310,12 +319,26 @@
     keep = attend_call(queries, False, F32)
     send = attend_call(theirs, True, BF16)
     conv_flops = 2 * owned * width * out_width * 3
-    taps_shape = decode_weight.shape[1:]
-    end_weight, held = call(
+    half_taps = (decode_weight.shape[1], width, out_width)
+    plane = (owned, out_width)
+    frame_far, frame_rest = call(
+        frame_kernel,
+        (S(plane, F32), S((2, *plane), F32)),
+        (frame, decode_weight),
+        far=(0, 1),
+        scratch=(
+            pltpu.VMEM(frame.shape, BF16),
+            pltpu.VMEM(half_taps, BF16),
+            pltpu.VMEM((2, *half_taps), BF16),
+            dma((4,)),
+        ),
+        flops=3 * conv_flops,
+    )
+    far_weight, rest_weight = call(
         stage_kernel,
-        (S((2, *taps_shape), BF16), S(frame.shape, BF16)),
-        (decode_weight, frame),
-        far=(0, 1),
+        (S(half_taps, BF16), S((2, *half_taps), BF16)),
+        (decode_weight,),
+        far=(0,),
         scratch=(dma((3,)),),
     )
     rows = width
@@ -335,28 +358,26 @@
             flops=3 * rows * lanes,
         )
         rows = out_rows - PAD
-    joined = call(
+    readout, far = call(
         functools.partial(readout_kernel, rows),
-        S((owned, 2 * width), BF16),
-        (keep, got, held),
-        flops=3 * rows * lanes,
-    )
-    far = far_by(joined)
-    near = near_by(joined)
-    part = call(
-        mid_conv_kernel,
-        S((owned, out_width), F32),
-        (joined, decode_weight),
-        far=(1,),
-        scratch=(pltpu.VMEM(taps_shape, BF16), dma((1,))),
+        (S((owned, width), BF16), S(plane, F32)),
+        (keep, got, frame_far, far_weight),
+        flops=conv_flops,
+    )
+    far = far_by(far)
+    near, middle = call(
+        rest_kernel,
+        (S(plane, F32), S(plane, F32)),
+        (readout, frame_rest, rest_weight),
         flops=2 * conv_flops,
     )
+    near = near_by(near)
     objects = mask_weight.shape[1]
     logits = call(
         functools.partial(last_kernel, count),
         S((objects, owned), F32),
-        (part, near, far, end_weight, mask_weight.T),
-        flops=4 * conv_flops,
+        (middle, near, far, mask_weight.T),
+        flops=2 * owned * out_width * objects,
     )
     return logits.T.reshape(query_value.shape[0], query_value.shape[1], objects)
 

time: 43.9 us -> 42.1 us (0.959)
  starting transfers between devices: 17 us -> 15.7 us
    ppermute x6, waiting for transfers between devices: 14.3 us -> 12.9 us  [swap(): return lax.ppermute(x, 'mem', [(i, i ^ order[step]) for i in range(count)])]
    ppermute x2, starting transfers between devices: 8.04 us -> 6.65 us  [near_by(): return lax.ppermute(x, 'mem', [(i, i ^ 1) for i in range(count)])]
    ppermute x1, waiting for transfers between devices: 2.27 us -> 3.32 us  [far_by(): return lax.ppermute(x, ('groups', 'mem'), links)]
    pallas_call x11 -> x12, Pallas kernels: 8.89 us -> 8.75 us  [call(): pl.pallas_call(kernel, out_shape=out, in_specs=[HB if i in far else SM if...]
where the time goes in v3:
time: 42.1 us; the launch traced here: 41.4 us
  waiting for transfers between devices  16.2 us (38%)
  starting transfers between devices  15.7 us (37%)
  Pallas kernels  8.75 us (21%)
  between operations  0.75 us (2%)
    ppermute x6, waiting for transfers between devices, swap(): return lax.ppermute(x, 'mem', [(i, i ^ order[step]) for i in range(count)])  12.9 us
    pallas_call x12, Pallas kernels, call(): pl.pallas_call(kernel, out_shape=out, in_specs=[HB if i in far else SM if...  8.75 us
    ppermute x6, starting transfers between devices, swap(): return lax.ppermute(x, 'mem', [(i, i ^ order[step]) for i in range(count)])  7.75 us
    ppermute x2, starting transfers between devices, near_by(): return lax.ppermute(x, 'mem', [(i, i ^ 1) for i in range(count)])  6.65 us
    ppermute x1, waiting for transfers between devices, far_by(): return lax.ppermute(x, ('groups', 'mem'), links)  3.32 us
    ppermute x1, starting transfers between devices, far_by(): return lax.ppermute(x, ('groups', 'mem'), links)  1.27 us
  transfers between devices with their start and end apart: 9, of which 6 were waited for; matrix products, arithmetic and copies ran while one was open for 0% of the time, Pallas kernels for 11%

profile of v3, /device:TPU:5, one launch (start us, length us, event | category | flops | bytes accessed | tf_op | source)
XLA Modules:
  0.0 41.4 jit_solution(1916476264812130236)
XLA Ops:
  0.7 1.6 %shard_map.91 = (bf16[528,640]{1,0:T(8,128)(2,1)S(1)}, bf16[64,128]{1,0:T(8,128)(2,1)S(1)}) custom-call(bf16[512,128]{1,0:T(8,128)(2,1)} %bitcast.10, bf16[512,512]{1,0:T(8,128)(2,1)} %bitcast.9, s32[4,128]{1,0:T(4,128)} %lab_hbm.1, bf16[8,512]{1,0:T(8,128)(2,1)} %emb_hbm.1, bf16[64,128]{1,0:T(8,128)(2,1)} %bitcast.12, s32[1]{0:T(128)S(6)} %copy.10.count_ref), custom_call_target="tpu_custom_call" | custom-call | flops 4194304 | bytes 1374212 | tf_op jit(solution)/shard_map/pallas_call | solution.py:27
  2.3 0.7 %collective-permute-start = (bf16[528,640]{1,0:T(8,128)(2,1)S(1)}, bf16[528,640]{1,0:T(8,128)(2,1)S(1)}, u32[]{:S(2)}, u32[]{:S(2)}) collective-permute-start(bf16[528,640]{1,0:T(8,128)(2,1)S(1)} %get-tuple-element.19.mine_ref), channel_id=1, source_target_pairs={{0,1},{1,0},{2,3},{3,2},{4,5},{5,4},{6,7},{7,6},{8,9},{9,8},{10,11... | collective-permute-start | bytes 2027528 | tf_op jit(solution)/shard_map/ppermute | solution.py:265
  3.0 2.3 %collective-permute-start.1 = (bf16[64,128]{1,0:T(8,128)(2,1)}, bf16[64,128]{1,0:T(8,128)(2,1)S(1)}, u32[]{:S(2)}, u32[]{:S(2)}) collective-permute-start(bf16[64,128]{1,0:T(8,128)(2,1)} %bitcast.13), channel_id=1, source_target_pairs={{0,8},{1,9},{2,10},{3,11},{4,12},{5,13},{6,14},{7,15},{8,0},{9,1},... | collective-permute-start | bytes 49160 | tf_op jit(solution)/shard_map/ppermute | solution.py:262
  5.3 1.4 %collective-permute-done.1.b_ref = bf16[64,128]{1,0:T(8,128)(2,1)S(1)} collective-permute-done((bf16[64,128]{1,0:T(8,128)(2,1)}, bf16[64,128]{1,0:T(8,128)(2,1)S(1)}, u32[]{:S(2)}, u32[]{:S(2)}) %collective-permute-start.1) | collective-permute-done | bytes 16416 | tf_op jit(solution)/shard_map/ppermute | solution.py:262
  6.7 0.2 collective-permute-start.2
  6.9 2.6 %collective-permute-done.2.b_ref = bf16[128,128]{1,0:T(8,128)(2,1)S(1)} collective-permute-done((bf16[128,128]{1,0:T(8,128)(2,1)S(1)}, bf16[128,128]{1,0:T(8,128)(2,1)S(1)}, u32[]{:S(2)}, u32[]{:S(2)}) %collective-permute-start.2) | collective-permute-done | bytes 32800 | tf_op jit(solution)/shard_map/ppermute | solution.py:262
  9.5 1.3 %collective-permute-start.3 = (bf16[256,128]{1,0:T(8,128)(2,1)S(1)}, bf16[256,128]{1,0:T(8,128)(2,1)S(1)}, u32[]{:S(2)}, u32[]{:S(2)}) collective-permute-start(bf16[256,128]{1,0:T(8,128)(2,1)S(1)} %shard_map.93.q_ref), channel_id=1, source_target_pairs={{0,4},{1,5},{2,6},{3,7},{4,0},{5,1},{6,2},{7,3},{8,12},{9,13},{10,... | collective-permute-start | bytes 196616 | tf_op jit(solution)/shard_map/ppermute | solution.py:262
  10.8 1.8 %collective-permute-done.3.q_ref = bf16[256,128]{1,0:T(8,128)(2,1)S(1)} collective-permute-done((bf16[256,128]{1,0:T(8,128)(2,1)S(1)}, bf16[256,128]{1,0:T(8,128)(2,1)S(1)}, u32[]{:S(2)}, u32[]{:S(2)}) %collective-permute-start.3) | collective-permute-done | bytes 65568 | tf_op jit(solution)/shard_map/ppermute | solution.py:262
  12.6 0.0 collective-permute-done.other_ref
  12.6 0.9 %shard_map.95 = bf16[528,256]{1,0:T(8,128)(2,1)S(1)} custom-call(bf16[528,640]{1,0:T(8,128)(2,1)S(1)} %get-tuple-element.19.mine_ref, bf16[528,640]{1,0:T(8,128)(2,1)S(1)} %collective-permute-done.other_ref, bf16[256,128]{1,0:T(8,128)(2,1)S(1)} %collective-permute-done.3.q_ref), custom_call_target="tpu_custom_call" | custom-call | flops 335544320 | bytes 1687552 | tf_op jit(solution)/shard_map/pallas_call | solution.py:27
  13.5 1.4 %collective-permute-start.4 = (bf16[528,256]{1,0:T(8,128)(2,1)S(1)}, bf16[528,256]{1,0:T(8,128)(2,1)S(1)}, u32[]{:S(2)}, u32[]{:S(2)}) collective-permute-start(bf16[528,256]{1,0:T(8,128)(2,1)S(1)} %shard_map.95), channel_id=1, source_target_pairs={{0,4},{1,5},{2,6},{3,7},{4,0},{5,1},{6,2},{7,3},{8,12},{9,13},{10,... | collective-permute-start | bytes 811016 | tf_op jit(solution)/shard_map/ppermute | solution.py:262
  14.9 0.9 %shard_map.94.keep_ref = f32[528,256]{1,0:T(8,128)S(1)} custom-call(bf16[528,640]{1,0:T(8,128)(2,1)S(1)} %get-tuple-element.19.mine_ref, bf16[528,640]{1,0:T(8,128)(2,1)S(1)} %collective-permute-done.other_ref, bf16[256,128]{1,0:T(8,128)(2,1)S(1)} %shard_map.93.q_ref), custom_call_target="tpu_custom_call" | custom-call | flops 335544320 | bytes 1957888 | tf_op jit(solution)/shard_map/pallas_call | solution.py:27
  15.8 3.1 %collective-permute-done.4.got_ref = bf16[528,256]{1,0:T(8,128)(2,1)S(1)} collective-permute-done((bf16[528,256]{1,0:T(8,128)(2,1)S(1)}, bf16[528,256]{1,0:T(8,128)(2,1)S(1)}, u32[]{:S(2)}, u32[]{:S(2)}) %collective-permute-start.4) | collective-permute-done | bytes 270368 | tf_op jit(solution)/shard_map/ppermute | solution.py:262
  18.9 0.1 shard_map.96
  19.0 0.2 collective-permute-start.5
  19.2 4.0 %collective-permute-done.5.got_ref = bf16[528,128]{1,0:T(8,128)(2,1)S(1)} collective-permute-done((bf16[528,128]{1,0:T(8,128)(2,1)S(1)}, bf16[528,128]{1,0:T(8,128)(2,1)S(1)}, u32[]{:S(2)}, u32[]{:S(2)}) %collective-permute-start.5) | collective-permute-done | bytes 135200 | tf_op jit(solution)/shard_map/ppermute | solution.py:262
  23.1 0.1 shard_map.97
  23.3 2.4 %collective-permute-start.6 = (bf16[272,128]{1,0:T(8,128)(2,1)S(1)}, bf16[272,128]{1,0:T(8,128)(2,1)S(1)}, u32[]{:S(2)}, u32[]{:S(2)}) collective-permute-start(bf16[272,128]{1,0:T(8,128)(2,1)S(1)} %get-tuple-element.24), channel_id=1, source_target_pairs={{0,8},{1,9},{2,10},{3,11},{4,12},{5,13},{6,14},{7,15},{8,0},{9,1},... | collective-permute-start | bytes 208904 | tf_op jit(solution)/shard_map/ppermute | solution.py:262
  25.7 1.6 %shard_map.99 = (bf16[3,512,256]{2,1,0:T(8,128)(2,1)S(1)}, bf16[2,3,512,256]{3,2,1,0:T(8,128)(2,1)S(1)}) custom-call(bf16[3,3,1024,256]{3,2,1,0:T(8,128)(2,1)} %w_hbm.3), custom_call_target="tpu_custom_call" | custom-call | bytes 7077888 | tf_op jit(solution)/shard_map/pallas_call | solution.py:27
  27.3 0.0 copy-start
  27.3 2.1 %shard_map.98 = (f32[64,256]{1,0:T(8,128)S(1)}, f32[2,64,256]{2,1,0:T(8,128)S(1)}) custom-call(bf16[64,512]{1,0:T(8,128)(2,1)} %bitcast.11, bf16[3,3,1024,256]{3,2,1,0:T(8,128)(2,1)} %w_hbm.3), custom_call_target="tpu_custom_call" | custom-call | flops 150994944 | bytes 4980736 | tf_op jit(solution)/shard_map/pallas_call | solution.py:27
  29.4 0.0 collective-permute-done.6.got_ref
  29.4 0.3 shard_map.100
  29.7 0.4 shard_map.101
  30.1 5.9 %collective-permute-start.7 = (f32[64,256]{1,0:T(8,128)S(1)}, f32[64,256]{1,0:T(8,128)S(1)}, u32[]{:S(2)}, u32[]{:S(2)}) collective-permute-start(f32[64,256]{1,0:T(8,128)S(1)} %get-tuple-element.31), channel_id=1, source_target_pairs={{0,1},{1,0},{2,3},{3,2},{4,5},{5,4},{6,7},{7,6},{8,9},{9,8},{10,11... | collective-permute-start | bytes 196616 | tf_op jit(solution)/shard_map/ppermute | solution.py:265
  36.0 1.3 %collective-permute-start.8 = (f32[64,256]{1,0:T(8,128)S(1)}, f32[64,256]{1,0:T(8,128)S(1)}, u32[]{:S(2)}, u32[]{:S(2)}) collective-permute-start(f32[64,256]{1,0:T(8,128)S(1)} %get-tuple-element.32), channel_id=1, source_target_pairs={{1,2},{3,4},{5,6},{7,8},{9,10},{11,12},{13,14},{0,16},{15,31},{17,... | collective-permute-start | bytes 196616 | tf_op jit(solution)/shard_map/ppermute | solution.py:275
  37.3 0.0 collective-permute-done.7.near_ref
  37.3 3.3 %collective-permute-done.8.far_ref = f32[64,256]{1,0:T(8,128)S(1)} collective-permute-done((f32[64,256]{1,0:T(8,128)S(1)}, f32[64,256]{1,0:T(8,128)S(1)}, u32[]{:S(2)}, u32[]{:S(2)}) %collective-permute-start.8) | collective-permute-done | bytes 65568 | tf_op jit(solution)/shard_map/ppermute | solution.py:275
  40.6 0.0 copy-done
  40.6 0.7 %shard_map.102 = f32[8,64]{1,0:T(8,128)} custom-call(f32[64,256]{1,0:T(8,128)S(1)} %get-tuple-element.30.mid_ref, f32[64,256]{1,0:T(8,128)S(1)} %collective-permute-done.7.near_ref, f32[64,256]{1,0:T(8,128)S(1)} %collective-permute-done.8.far_ref, bf16[8,256]{1,0:T(8,128)(2,1)S(1)} %bitcast.8), custom_call_target="tpu_custom_call" | custom-call | flops 262144 | bytes 202752 | tf_op jit(solution)/shard_map/pallas_call | solution.py:27
  (2 shorter events, 0.0 us)
Async XLA Ops:
  2.3 10.3 %collective-permute-start = (bf16[528,640]{1,0:T(8,128)(2,1)S(1)}, bf16[528,640]{1,0:T(8,128)(2,1)S(1)}, u32[]{:S(2)}, u32[]{:S(2)}) collective-permute-start(bf16[528,640]{1,0:T(8,128)(2,1)S(1)} %get-tuple-element.19.mine_ref), channel_id=1, source_target_pairs={{0,1},{1,0},{2,3},{3,2},{4,5},{5,4},{6,7},{7,6},{8,9},{9,8},{10,11... | collective-permute-start | bytes 2027528 | tf_op jit(solution)/shard_map/ppermute | solution.py:265
  3.0 3.7 %collective-permute-start.1 = (bf16[64,128]{1,0:T(8,128)(2,1)}, bf16[64,128]{1,0:T(8,128)(2,1)S(1)}, u32[]{:S(2)}, u32[]{:S(2)}) collective-permute-start(bf16[64,128]{1,0:T(8,128)(2,1)} %bitcast.13), channel_id=1, source_target_pairs={{0,8},{1,9},{2,10},{3,11},{4,12},{5,13},{6,14},{7,15},{8,0},{9,1},... | collective-permute-start | bytes 49160 | tf_op jit(solution)/shard_map/ppermute | solution.py:262
  6.7 2.8 %collective-permute-start.2 = (bf16[128,128]{1,0:T(8,128)(2,1)S(1)}, bf16[128,128]{1,0:T(8,128)(2,1)S(1)}, u32[]{:S(2)}, u32[]{:S(2)}) collective-permute-start(bf16[128,128]{1,0:T(8,128)(2,1)S(1)} %shard_map.92.a_ref), channel_id=1, source_target_pairs={{0,2},{1,3},{2,0},{3,1},{4,6},{5,7},{6,4},{7,5},{8,10},{9,11},{10,... | collective-permute-start | bytes 98312 | tf_op jit(solution)/shard_map/ppermute | solution.py:262
  9.5 3.1 %collective-permute-start.3 = (bf16[256,128]{1,0:T(8,128)(2,1)S(1)}, bf16[256,128]{1,0:T(8,128)(2,1)S(1)}, u32[]{:S(2)}, u32[]{:S(2)}) collective-permute-start(bf16[256,128]{1,0:T(8,128)(2,1)S(1)} %shard_map.93.q_ref), channel_id=1, source_target_pairs={{0,4},{1,5},{2,6},{3,7},{4,0},{5,1},{6,2},{7,3},{8,12},{9,13},{10,... | collective-permute-start | bytes 196616 | tf_op jit(solution)/shard_map/ppermute | solution.py:262
  13.5 5.4 %collective-permute-start.4 = (bf16[528,256]{1,0:T(8,128)(2,1)S(1)}, bf16[528,256]{1,0:T(8,128)(2,1)S(1)}, u32[]{:S(2)}, u32[]{:S(2)}) collective-permute-start(bf16[528,256]{1,0:T(8,128)(2,1)S(1)} %shard_map.95), channel_id=1, source_target_pairs={{0,4},{1,5},{2,6},{3,7},{4,0},{5,1},{6,2},{7,3},{8,12},{9,13},{10,... | collective-permute-start | bytes 811016 | tf_op jit(solution)/shard_map/ppermute | solution.py:262
  19.0 4.2 %collective-permute-start.5 = (bf16[528,128]{1,0:T(8,128)(2,1)S(1)}, bf16[528,128]{1,0:T(8,128)(2,1)S(1)}, u32[]{:S(2)}, u32[]{:S(2)}) collective-permute-start(bf16[528,128]{1,0:T(8,128)(2,1)S(1)} %get-tuple-element.22), channel_id=1, source_target_pairs={{0,2},{1,3},{2,0},{3,1},{4,6},{5,7},{6,4},{7,5},{8,10},{9,11},{10,... | collective-permute-start | bytes 405512 | tf_op jit(solution)/shard_map/ppermute | solution.py:262
  23.3 6.1 %collective-permute-start.6 = (bf16[272,128]{1,0:T(8,128)(2,1)S(1)}, bf16[272,128]{1,0:T(8,128)(2,1)S(1)}, u32[]{:S(2)}, u32[]{:S(2)}) collective-permute-start(bf16[272,128]{1,0:T(8,128)(2,1)S(1)} %get-tuple-element.24), channel_id=1, source_target_pairs={{0,8},{1,9},{2,10},{3,11},{4,12},{5,13},{6,14},{7,15},{8,0},{9,1},... | collective-permute-start | bytes 208904 | tf_op jit(solution)/shard_map/ppermute | solution.py:262
  27.3 13.3 %copy-start = (bf16[256,8]{0,1:T(8,128)(2,1)S(1)}, bf16[256,8]{0,1:T(8,128)(2,1)}, u32[]{:S(2)}) copy-start(bf16[256,8]{0,1:T(8,128)(2,1)} %param.17) | copy-start | bytes 12292
  30.1 7.2 %collective-permute-start.7 = (f32[64,256]{1,0:T(8,128)S(1)}, f32[64,256]{1,0:T(8,128)S(1)}, u32[]{:S(2)}, u32[]{:S(2)}) collective-permute-start(f32[64,256]{1,0:T(8,128)S(1)} %get-tuple-element.31), channel_id=1, source_target_pairs={{0,1},{1,0},{2,3},{3,2},{4,5},{5,4},{6,7},{7,6},{8,9},{9,8},{10,11... | collective-permute-start | bytes 196616 | tf_op jit(solution)/shard_map/ppermute | solution.py:265
  36.0 4.6 %collective-permute-start.8 = (f32[64,256]{1,0:T(8,128)S(1)}, f32[64,256]{1,0:T(8,128)S(1)}, u32[]{:S(2)}, u32[]{:S(2)}) collective-permute-start(f32[64,256]{1,0:T(8,128)S(1)} %get-tuple-element.32), channel_id=1, source_target_pairs={{1,2},{3,4},{5,6},{7,8},{9,10},{11,12},{13,14},{0,16},{15,31},{17,... | collective-permute-start | bytes 196616 | tf_op jit(solution)/shard_map/ppermute | solution.py:275

commit v4 on v3

--- a/solution.py
+++ b/solution.py
@@ -12,6 +12,7 @@
 F32 = jnp.float32
 BF16 = jnp.bfloat16
 PAD = 16
+BLOCK = 128
 VM = pl.BlockSpec(memory_space=pltpu.VMEM)
 SM = pl.BlockSpec(memory_space=pltpu.SMEM)
 HB = pl.BlockSpec(memory_space=pl.ANY)
@@ -111,7 +112,10 @@
 
 
 def attend_kernel(pos, kwidth, width, send, mine_ref, other_ref, q_ref, out_ref):
-    peak, values = attend((mine_ref, other_ref), q_ref[...], pos, kwidth, width)
+    starts = range(BLOCK * send, q_ref.shape[0], 2 * BLOCK)
+    queries = [q_ref[i : i + BLOCK] for i in starts]
+    queries = queries[0] if len(queries) == 1 else jnp.concatenate(queries, axis=0)
+    peak, values = attend((mine_ref, other_ref), queries, pos, kwidth, width)
     mass = values[width : width + 1]
     out_ref[0:width] = values[0:width].astype(out_ref.dtype)
     out_ref[width : width + PAD] = (pack_tail if send else keep_tail)(peak, mass)
@@ -128,26 +132,51 @@
     return values, top, mass * a + got_mass * b
 
 
+def put(width, send_out, keep_out, sent, kept):
+    send_out[0:width] = sent[0].astype(BF16)
+    send_out[width : width + PAD] = pack_tail(*sent[1:])
+    keep_out[0:width] = kept[0]
+    keep_out[width : width + PAD] = keep_tail(*kept[1:])
+
+
+def first_fold_kernel(width, keep0_ref, got0_ref, keep1_ref, got1_ref, send_out, keep_out):
+    early = merged(width, keep0_ref, got0_ref)
+    late = merged(width, keep1_ref, got1_ref)
+    half = BLOCK // 2
+    lane = lax.broadcasted_iota(jnp.int32, (1, BLOCK), 1) < half
+    kept, sent = [], []
+    for a, b in zip(early, late, strict=True):
+        rows = a.shape[0]
+        wide = max(rows, 8)
+        a, b = (jnp.broadcast_to(x, (wide, x.shape[1])) for x in (a, b))
+        low, high = [], []
+        for i in range(0, a.shape[1], BLOCK):
+            left, right = a[:, i : i + BLOCK], b[:, i : i + BLOCK]
+            low.append(jnp.where(lane, left, pltpu.roll(right, half, 1)))
+            high.append(jnp.where(lane, pltpu.roll(left, half, 1), right))
+        join = lambda xs: (xs[0] if len(xs) == 1 else jnp.concatenate(xs, axis=1))[0:rows]
+        kept.append(join(low))
+        sent.append(join(high))
+    put(width, send_out, keep_out, sent, kept)
+
+
 def fold_kernel(width, keep_ref, got_ref, send_out, keep_out):
     values, peak, mass = merged(width, keep_ref, got_ref)
     half = values.shape[1] // 2
-    if half % 128 == 0:
-        send_out[0:width] = values[:, half:].astype(BF16)
-        send_out[width : width + PAD] = pack_tail(peak[:, half:], mass[:, half:])
-        keep_out[0:width] = values[:, :half]
-        keep_out[width : width + PAD] = keep_tail(peak[:, :half], mass[:, :half])
+    if half % BLOCK == 0:
+        sent, kept = (tuple(x[:, i : i + half] for x in (values, peak, mass)) for i in (half, 0))
+        put(width, send_out, keep_out, sent, kept)
         return
     rows = width // 2
     low, high = values[0:rows], values[rows:]
     lane = lax.broadcasted_iota(jnp.int32, (1, 2 * half), 1) < half
     swap = lambda x: pltpu.roll(x, half, 1)
-    first = lambda x: jnp.where(lane, x, swap(x))
-    second = lambda x: jnp.where(lane, swap(x), x)
     peak8, mass8 = (jnp.broadcast_to(x, (8, 2 * half)) for x in (peak, mass))
-    send_out[0:rows] = jnp.where(lane, swap(low), high).astype(BF16)
-    send_out[rows : rows + PAD] = pack_tail(second(peak8)[0:1], second(mass8)[0:1])
-    keep_out[0:rows] = jnp.where(lane, low, swap(high))
-    keep_out[rows : rows + PAD] = keep_tail(first(peak8)[0:1], first(mass8)[0:1])
+    second = lambda x: jnp.where(lane, swap(x), x)[0:1]
+    first = lambda x: jnp.where(lane, x, swap(x))[0:1]
+    sent = (jnp.where(lane, swap(low), high), second(peak8), second(mass8))
+    kept = (jnp.where(lane, low, swap(high)), first(peak8), first(mass8))
+    put(rows, send_out, keep_out, sent, kept)
 
 
 def far_row():
@@ -254,12 +283,11 @@
     owned = query_value.shape[0] * query_value.shape[1]
     out_width = decode_weight.shape[3]
 
-    steps = count.bit_length() - 2
-    order = [1 << i for i in range(1, steps + 1)]
-    order[0:2] = order[1::-1]
-
-    def swap(x, step):
-        return lax.ppermute(x, "mem", [(i, i ^ order[step]) for i in range(count)])
+    gathers = [1 << i for i in range(1, count.bit_length() - 1)]
+    reduces = [gathers[1], gathers[0], *gathers[2:]]
+
+    def swap(x, mask):
+        return lax.ppermute(x, "mem", [(i, i ^ mask) for i in range(count)])
 
     def near_by(x):
         return lax.ppermute(x, "mem", [(i, i ^ 1) for i in range(count)])
@@ -277,7 +305,7 @@
     queries = query_key.reshape(owned, kwidth)
     frame = query_value.reshape(owned, width)
     dma = pltpu.SemaphoreType.DMA
-    got = swap(queries, steps - 1)
+    got = swap(queries, gathers[0])
     mine, queries = call(
         prep_kernel,
         (S((tall, pos + kwidth), BF16), S(queries.shape, BF16)),
@@ -301,23 +329,28 @@
     )
     other = near_by(mine)
 
-    for i in range(steps - 1):
+    for mask in gathers[1:]:
         queries = call(
             join_kernel, S((2 * queries.shape[0], kwidth), BF16), (queries, got)
         )
-        got = swap(queries, steps - 2 - i)
-    theirs = got
-
-    lanes = queries.shape[0]
-    work = dict(flops=4 * lanes * pos * (kwidth + width), exps=2 * lanes * pos)
-    attend_call = lambda q, send, dtype: call(
-        functools.partial(attend_kernel, pos, kwidth, width, send),
-        S((width + PAD, lanes), dtype),
-        (mine, other, q),
-        **work,
-    )
-    keep = attend_call(queries, False, F32)
-    send = attend_call(theirs, True, BF16)
+        got = swap(queries, mask)
+
+    lanes = queries.shape[0] // 2
+    keeps, gots = [], []
+    for block in (queries, got):
+        sides = []
+        for send, dtype in ((1, BF16), (0, F32)):
+            sides.append(
+                call(
+                    functools.partial(attend_kernel, pos, kwidth, width, send),
+                    S((width + PAD, lanes), dtype),
+                    (mine, other, block),
+                    flops=4 * lanes * pos * (kwidth + width),
+                    exps=2 * lanes * pos,
+                )
+            )
+        gots.append(swap(sides[0], reduces[0]))
+        keeps.append(sides[1])
     conv_flops = 2 * owned * width * out_width * 3
     half_taps = (decode_weight.shape[1], width, out_width)
     plane = (owned, out_width)
@@ -341,13 +374,19 @@
         far=(0,),
         scratch=(dma((3,)),),
     )
+    send, keep = call(
+        functools.partial(first_fold_kernel, width),
+        (S((width + PAD, lanes), BF16), S((width + PAD, lanes), F32)),
+        (keeps[0], gots[0], keeps[1], gots[1]),
+        flops=6 * width * lanes,
+    )
     rows = width
-    for i in range(steps):
-        got = swap(send, i)
-        if i + 1 == steps:
+    for mask in reduces[1:]:
+        got = swap(send, mask)
+        if mask == reduces[-1]:
             break
         lanes = lanes // 2
-        if lanes % 128:
+        if lanes % BLOCK:
             out_rows, out_lanes = rows // 2 + PAD, 2 * lanes
         else:
             out_rows, out_lanes = rows + PAD, lanes

time: 42.1 us -> 41.3 us (0.981)
  waiting for transfers between devices: 16.2 us -> 13.5 us
  Pallas kernels: 8.75 us -> 10 us
  starting transfers between devices: 15.7 us -> 16.3 us
    ppermute x6 -> x7, waiting for transfers between devices: 12.9 us -> 10.2 us  [swap(): return lax.ppermute(x, 'mem', [(i, i ^ mask) for i in range(count)])]
    pallas_call x12 -> x14, Pallas kernels: 8.75 us -> 10 us  [call(): pl.pallas_call(kernel, out_shape=out, in_specs=[HB if i in far else SM if...]
    ppermute x6 -> x7, starting transfers between devices: 7.75 us -> 8.27 us  [swap(): return lax.ppermute(x, 'mem', [(i, i ^ mask) for i in range(count)])]
  transfers between devices with their start and end apart: 9 -> 10, of which waited for: 6 -> 5; matrix products, arithmetic and copies ran while one was open for 0% -> 0% of each run, Pallas kernels for 11% -> 16%
where the time goes in v4:
time: 41.3 us; the launch traced here: 40.6 us
  starting transfers between devices  16.3 us (39%)
  waiting for transfers between devices  13.5 us (33%)
  Pallas kernels  10 us (24%)
  between operations  0.75 us (2%)
    ppermute x7, waiting for transfers between devices, swap(): return lax.ppermute(x, 'mem', [(i, i ^ mask) for i in range(count)])  10.2 us
    pallas_call x14, Pallas kernels, call(): pl.pallas_call(kernel, out_shape=out, in_specs=[HB if i in far else SM if...  10 us
    ppermute x7, starting transfers between devices, swap(): return lax.ppermute(x, 'mem', [(i, i ^ mask) for i in range(count)])  8.27 us
    ppermute x2, starting transfers between devices, near_by(): return lax.ppermute(x, 'mem', [(i, i ^ 1) for i in range(count)])  6.76 us
    ppermute x1, waiting for transfers between devices, far_by(): return lax.ppermute(x, ('groups', 'mem'), links)  3.34 us
    ppermute x1, starting transfers between devices, far_by(): return lax.ppermute(x, ('groups', 'mem'), links)  1.25 us
  transfers between devices with their start and end apart: 10, of which 5 were waited for; matrix products, arithmetic and copies ran while one was open for 0% of the time, Pallas kernels for 16%

profile of v4, /device:TPU:5, one launch (start us, length us, event | category | flops | bytes accessed | tf_op | source)
XLA Modules:
  0.0 40.6 jit_solution(10380695905874209643)
XLA Ops:
  0.7 1.6 %shard_map.91 = (bf16[528,640]{1,0:T(8,128)(2,1)S(1)}, bf16[64,128]{1,0:T(8,128)(2,1)S(1)}) custom-call(bf16[512,128]{1,0:T(8,128)(2,1)} %bitcast.10, bf16[512,512]{1,0:T(8,128)(2,1)} %bitcast.9, s32[4,128]{1,0:T(4,128)} %lab_hbm.1, bf16[8,512]{1,0:T(8,128)(2,1)} %emb_hbm.1, bf16[64,128]{1,0:T(8,128)(2,1)} %bitcast.12, s32[1]{0:T(128)S(6)} %copy.10.count_ref), custom_call_target="tpu_custom_call" | custom-call | flops 4194304 | bytes 1374212 | tf_op jit(solution)/shard_map/pallas_call | solution.py:28
  2.3 0.7 %collective-permute-start = (bf16[528,640]{1,0:T(8,128)(2,1)S(1)}, bf16[528,640]{1,0:T(8,128)(2,1)S(1)}, u32[]{:S(2)}, u32[]{:S(2)}) collective-permute-start(bf16[528,640]{1,0:T(8,128)(2,1)S(1)} %get-tuple-element.19.mine_ref), channel_id=1, source_target_pairs={{0,1},{1,0},{2,3},{3,2},{4,5},{5,4},{6,7},{7,6},{8,9},{9,8},{10,11... | collective-permute-start | bytes 2027528 | tf_op jit(solution)/shard_map/ppermute | solution.py:293
  3.0 0.0 collective-permute-start.1
  3.0 2.8 %collective-permute-done.1.b_ref = bf16[64,128]{1,0:T(8,128)(2,1)S(1)} collective-permute-done((bf16[64,128]{1,0:T(8,128)(2,1)}, bf16[64,128]{1,0:T(8,128)(2,1)S(1)}, u32[]{:S(2)}, u32[]{:S(2)}) %collective-permute-start.1) | collective-permute-done | bytes 16416 | tf_op jit(solution)/shard_map/ppermute | solution.py:290
  5.8 1.3 %collective-permute-start.2 = (bf16[128,128]{1,0:T(8,128)(2,1)S(1)}, bf16[128,128]{1,0:T(8,128)(2,1)S(1)}, u32[]{:S(2)}, u32[]{:S(2)}) collective-permute-start(bf16[128,128]{1,0:T(8,128)(2,1)S(1)} %shard_map.92.a_ref), channel_id=1, source_target_pairs={{0,4},{1,5},{2,6},{3,7},{4,0},{5,1},{6,2},{7,3},{8,12},{9,13},{10,... | collective-permute-start | bytes 98312 | tf_op jit(solution)/shard_map/ppermute | solution.py:290
  7.1 1.5 %collective-permute-done.2.b_ref = bf16[128,128]{1,0:T(8,128)(2,1)S(1)} collective-permute-done((bf16[128,128]{1,0:T(8,128)(2,1)S(1)}, bf16[128,128]{1,0:T(8,128)(2,1)S(1)}, u32[]{:S(2)}, u32[]{:S(2)}) %collective-permute-start.2) | collective-permute-done | bytes 32800 | tf_op jit(solution)/shard_map/ppermute | solution.py:290
  8.6 2.3 %collective-permute-start.4 = (bf16[256,128]{1,0:T(8,128)(2,1)S(1)}, bf16[256,128]{1,0:T(8,128)(2,1)S(1)}, u32[]{:S(2)}, u32[]{:S(2)}) collective-permute-start(bf16[256,128]{1,0:T(8,128)(2,1)S(1)} %shard_map.93.q_ref), channel_id=1, source_target_pairs={{0,8},{1,9},{2,10},{3,11},{4,12},{5,13},{6,14},{7,15},{8,0},{9,1},... | collective-permute-start | bytes 196616 | tf_op jit(solution)/shard_map/ppermute | solution.py:290
  10.9 0.0 collective-permute-done.other_ref
  10.9 0.7 %shard_map.95 = bf16[528,128]{1,0:T(8,128)(2,1)S(1)} custom-call(bf16[528,640]{1,0:T(8,128)(2,1)S(1)} %get-tuple-element.19.mine_ref, bf16[528,640]{1,0:T(8,128)(2,1)S(1)} %collective-permute-done.other_ref, bf16[256,128]{1,0:T(8,128)(2,1)S(1)} %shard_map.93.q_ref), custom_call_target="tpu_custom_call" | custom-call | flops 167772160 | bytes 1552384 | tf_op jit(solution)/shard_map/pallas_call | solution.py:28
  11.6 1.4 %collective-permute-start.3 = (bf16[528,128]{1,0:T(8,128)(2,1)S(1)}, bf16[528,128]{1,0:T(8,128)(2,1)S(1)}, u32[]{:S(2)}, u32[]{:S(2)}) collective-permute-start(bf16[528,128]{1,0:T(8,128)(2,1)S(1)} %shard_map.95), channel_id=1, source_target_pairs={{0,4},{1,5},{2,6},{3,7},{4,0},{5,1},{6,2},{7,3},{8,12},{9,13},{10,... | collective-permute-start | bytes 405512 | tf_op jit(solution)/shard_map/ppermute | solution.py:290
  13.0 0.0 collective-permute-done.4.q_ref
  13.0 0.7 %shard_map.97 = bf16[528,128]{1,0:T(8,128)(2,1)S(1)} custom-call(bf16[528,640]{1,0:T(8,128)(2,1)S(1)} %get-tuple-element.19.mine_ref, bf16[528,640]{1,0:T(8,128)(2,1)S(1)} %collective-permute-done.other_ref, bf16[256,128]{1,0:T(8,128)(2,1)S(1)} %collective-permute-done.4.q_ref), custom_call_target="tpu_custom_call" | custom-call | flops 167772160 | bytes 1552384 | tf_op jit(solution)/shard_map/pallas_call | solution.py:28
  13.7 1.1 %collective-permute-start.5 = (bf16[528,128]{1,0:T(8,128)(2,1)S(1)}, bf16[528,128]{1,0:T(8,128)(2,1)S(1)}, u32[]{:S(2)}, u32[]{:S(2)}) collective-permute-start(bf16[528,128]{1,0:T(8,128)(2,1)S(1)} %shard_map.97), channel_id=1, source_target_pairs={{0,4},{1,5},{2,6},{3,7},{4,0},{5,1},{6,2},{7,3},{8,12},{9,13},{10,... | collective-permute-start | bytes 405512 | tf_op jit(solution)/shard_map/ppermute | solution.py:290
  14.8 0.7 %shard_map.94.keep0_ref = f32[528,128]{1,0:T(8,128)S(1)} custom-call(bf16[528,640]{1,0:T(8,128)(2,1)S(1)} %get-tuple-element.19.mine_ref, bf16[528,640]{1,0:T(8,128)(2,1)S(1)} %collective-permute-done.other_ref, bf16[256,128]{1,0:T(8,128)(2,1)S(1)} %shard_map.93.q_ref), custom_call_target="tpu_custom_call" | custom-call | flops 167772160 | bytes 1687552 | tf_op jit(solution)/shard_map/pallas_call | solution.py:28
  15.5 0.7 %shard_map.96.keep1_ref = f32[528,128]{1,0:T(8,128)S(1)} custom-call(bf16[528,640]{1,0:T(8,128)(2,1)S(1)} %get-tuple-element.19.mine_ref, bf16[528,640]{1,0:T(8,128)(2,1)S(1)} %collective-permute-done.other_ref, bf16[256,128]{1,0:T(8,128)(2,1)S(1)} %collective-permute-done.4.q_ref), custom_call_target="tpu_custom_call" | custom-call | flops 167772160 | bytes 1687552 | tf_op jit(solution)/shard_map/pallas_call | solution.py:28
  16.2 0.0 collective-permute-done.3.got0_ref
  16.3 2.2 %collective-permute-done.5.got1_ref = bf16[528,128]{1,0:T(8,128)(2,1)S(1)} collective-permute-done((bf16[528,128]{1,0:T(8,128)(2,1)S(1)}, bf16[528,128]{1,0:T(8,128)(2,1)S(1)}, u32[]{:S(2)}, u32[]{:S(2)}) %collective-permute-start.5) | collective-permute-done | bytes 135200 | tf_op jit(solution)/shard_map/ppermute | solution.py:290
  18.5 0.2 shard_map.98
  18.7 0.3 collective-permute-start.6
  18.9 3.7 %collective-permute-done.6.got_ref = bf16[528,128]{1,0:T(8,128)(2,1)S(1)} collective-permute-done((bf16[528,128]{1,0:T(8,128)(2,1)S(1)}, bf16[528,128]{1,0:T(8,128)(2,1)S(1)}, u32[]{:S(2)}, u32[]{:S(2)}) %collective-permute-start.6) | collective-permute-done | bytes 135200 | tf_op jit(solution)/shard_map/ppermute | solution.py:290
  22.6 0.1 shard_map.99
  22.8 2.0 %collective-permute-start.7 = (bf16[272,128]{1,0:T(8,128)(2,1)S(1)}, bf16[272,128]{1,0:T(8,128)(2,1)S(1)}, u32[]{:S(2)}, u32[]{:S(2)}) collective-permute-start(bf16[272,128]{1,0:T(8,128)(2,1)S(1)} %get-tuple-element.24), channel_id=1, source_target_pairs={{0,8},{1,9},{2,10},{3,11},{4,12},{5,13},{6,14},{7,15},{8,0},{9,1},... | collective-permute-start | bytes 208904 | tf_op jit(solution)/shard_map/ppermute | solution.py:290
  24.7 1.6 %shard_map.101 = (bf16[3,512,256]{2,1,0:T(8,128)(2,1)S(1)}, bf16[2,3,512,256]{3,2,1,0:T(8,128)(2,1)S(1)}) custom-call(bf16[3,3,1024,256]{3,2,1,0:T(8,128)(2,1)} %w_hbm.3), custom_call_target="tpu_custom_call" | custom-call | bytes 7077888 | tf_op jit(solution)/shard_map/pallas_call | solution.py:28
  26.4 0.0 copy-start
  26.4 2.1 %shard_map.100 = (f32[64,256]{1,0:T(8,128)S(1)}, f32[2,64,256]{2,1,0:T(8,128)S(1)}) custom-call(bf16[64,512]{1,0:T(8,128)(2,1)} %bitcast.11, bf16[3,3,1024,256]{3,2,1,0:T(8,128)(2,1)} %w_hbm.3), custom_call_target="tpu_custom_call" | custom-call | flops 150994944 | bytes 4980736 | tf_op jit(solution)/shard_map/pallas_call | solution.py:28
  28.5 0.0 collective-permute-done.7.got_ref
  28.5 0.3 shard_map.102
  28.8 0.4 shard_map.103
  29.2 6.0 %collective-permute-start.8 = (f32[64,256]{1,0:T(8,128)S(1)}, f32[64,256]{1,0:T(8,128)S(1)}, u32[]{:S(2)}, u32[]{:S(2)}) collective-permute-start(f32[64,256]{1,0:T(8,128)S(1)} %get-tuple-element.31), channel_id=1, source_target_pairs={{0,1},{1,0},{2,3},{3,2},{4,5},{5,4},{6,7},{7,6},{8,9},{9,8},{10,11... | collective-permute-start | bytes 196616 | tf_op jit(solution)/shard_map/ppermute | solution.py:293
  35.2 1.2 %collective-permute-start.9 = (f32[64,256]{1,0:T(8,128)S(1)}, f32[64,256]{1,0:T(8,128)S(1)}, u32[]{:S(2)}, u32[]{:S(2)}) collective-permute-start(f32[64,256]{1,0:T(8,128)S(1)} %get-tuple-element.32), channel_id=1, source_target_pairs={{1,2},{3,4},{5,6},{7,8},{9,10},{11,12},{13,14},{0,16},{15,31},{17,... | collective-permute-start | bytes 196616 | tf_op jit(solution)/shard_map/ppermute | solution.py:303
  36.5 0.0 collective-permute-done.8.near_ref
  36.5 3.3 %collective-permute-done.9.far_ref = f32[64,256]{1,0:T(8,128)S(1)} collective-permute-done((f32[64,256]{1,0:T(8,128)S(1)}, f32[64,256]{1,0:T(8,128)S(1)}, u32[]{:S(2)}, u32[]{:S(2)}) %collective-permute-start.9) | collective-permute-done | bytes 65568 | tf_op jit(solution)/shard_map/ppermute | solution.py:303
  39.8 0.0 copy-done
  39.8 0.7 %shard_map.104 = f32[8,64]{1,0:T(8,128)} custom-call(f32[64,256]{1,0:T(8,128)S(1)} %get-tuple-element.30.mid_ref, f32[64,256]{1,0:T(8,128)S(1)} %collective-permute-done.8.near_ref, f32[64,256]{1,0:T(8,128)S(1)} %collective-permute-done.9.far_ref, bf16[8,256]{1,0:T(8,128)(2,1)S(1)} %bitcast.8), custom_call_target="tpu_custom_call" | custom-call | flops 262144 | bytes 202752 | tf_op jit(solution)/shard_map/pallas_call | solution.py:28
  (2 shorter events, 0.0 us)
Async XLA Ops:
  2.3 8.6 %collective-permute-start = (bf16[528,640]{1,0:T(8,128)(2,1)S(1)}, bf16[528,640]{1,0:T(8,128)(2,1)S(1)}, u32[]{:S(2)}, u32[]{:S(2)}) collective-permute-start(bf16[528,640]{1,0:T(8,128)(2,1)S(1)} %get-tuple-element.19.mine_ref), channel_id=1, source_target_pairs={{0,1},{1,0},{2,3},{3,2},{4,5},{5,4},{6,7},{7,6},{8,9},{9,8},{10,11... | collective-permute-start | bytes 2027528 | tf_op jit(solution)/shard_map/ppermute | solution.py:293
  3.0 2.8 %collective-permute-start.1 = (bf16[64,128]{1,0:T(8,128)(2,1)}, bf16[64,128]{1,0:T(8,128)(2,1)S(1)}, u32[]{:S(2)}, u32[]{:S(2)}) collective-permute-start(bf16[64,128]{1,0:T(8,128)(2,1)} %bitcast.13), channel_id=1, source_target_pairs={{0,2},{1,3},{2,0},{3,1},{4,6},{5,7},{6,4},{7,5},{8,10},{9,11},{10,... | collective-permute-start | bytes 49160 | tf_op jit(solution)/shard_map/ppermute | solution.py:290
  5.8 2.8 %collective-permute-start.2 = (bf16[128,128]{1,0:T(8,128)(2,1)S(1)}, bf16[128,128]{1,0:T(8,128)(2,1)S(1)}, u32[]{:S(2)}, u32[]{:S(2)}) collective-permute-start(bf16[128,128]{1,0:T(8,128)(2,1)S(1)} %shard_map.92.a_ref), channel_id=1, source_target_pairs={{0,4},{1,5},{2,6},{3,7},{4,0},{5,1},{6,2},{7,3},{8,12},{9,13},{10,... | collective-permute-start | bytes 98312 | tf_op jit(solution)/shard_map/ppermute | solution.py:290
  8.6 4.4 %collective-permute-start.4 = (bf16[256,128]{1,0:T(8,128)(2,1)S(1)}, bf16[256,128]{1,0:T(8,128)(2,1)S(1)}, u32[]{:S(2)}, u32[]{:S(2)}) collective-permute-start(bf16[256,128]{1,0:T(8,128)(2,1)S(1)} %shard_map.93.q_ref), channel_id=1, source_target_pairs={{0,8},{1,9},{2,10},{3,11},{4,12},{5,13},{6,14},{7,15},{8,0},{9,1},... | collective-permute-start | bytes 196616 | tf_op jit(solution)/shard_map/ppermute | solution.py:290
  11.6 4.6 %collective-permute-start.3 = (bf16[528,128]{1,0:T(8,128)(2,1)S(1)}, bf16[528,128]{1,0:T(8,128)(2,1)S(1)}, u32[]{:S(2)}, u32[]{:S(2)}) collective-permute-start(bf16[528,128]{1,0:T(8,128)(2,1)S(1)} %shard_map.95), channel_id=1, source_target_pairs={{0,4},{1,5},{2,6},{3,7},{4,0},{5,1},{6,2},{7,3},{8,12},{9,13},{10,... | collective-permute-start | bytes 405512 | tf_op jit(solution)/shard_map/ppermute | solution.py:290
  13.7 4.8 %collective-permute-start.5 = (bf16[528,128]{1,0:T(8,128)(2,1)S(1)}, bf16[528,128]{1,0:T(8,128)(2,1)S(1)}, u32[]{:S(2)}, u32[]{:S(2)}) collective-permute-start(bf16[528,128]{1,0:T(8,128)(2,1)S(1)} %shard_map.97), channel_id=1, source_target_pairs={{0,4},{1,5},{2,6},{3,7},{4,0},{5,1},{6,2},{7,3},{8,12},{9,13},{10,... | collective-permute-start | bytes 405512 | tf_op jit(solution)/shard_map/ppermute | solution.py:290
  18.7 3.9 %collective-permute-start.6 = (bf16[528,128]{1,0:T(8,128)(2,1)S(1)}, bf16[528,128]{1,0:T(8,128)(2,1)S(1)}, u32[]{:S(2)}, u32[]{:S(2)}) collective-permute-start(bf16[528,128]{1,0:T(8,128)(2,1)S(1)} %get-tuple-element.22), channel_id=1, source_target_pairs={{0,2},{1,3},{2,0},{3,1},{4,6},{5,7},{6,4},{7,5},{8,10},{9,11},{10,... | collective-permute-start | bytes 405512 | tf_op jit(solution)/shard_map/ppermute | solution.py:290
  22.8 5.7 %collective-permute-start.7 = (bf16[272,128]{1,0:T(8,128)(2,1)S(1)}, bf16[272,128]{1,0:T(8,128)(2,1)S(1)}, u32[]{:S(2)}, u32[]{:S(2)}) collective-permute-start(bf16[272,128]{1,0:T(8,128)(2,1)S(1)} %get-tuple-element.24), channel_id=1, source_target_pairs={{0,8},{1,9},{2,10},{3,11},{4,12},{5,13},{6,14},{7,15},{8,0},{9,1},... | collective-permute-start | bytes 208904 | tf_op jit(solution)/shard_map/ppermute | solution.py:290
  26.4 13.4 %copy-start = (bf16[256,8]{0,1:T(8,128)(2,1)S(1)}, bf16[256,8]{0,1:T(8,128)(2,1)}, u32[]{:S(2)}) copy-start(bf16[256,8]{0,1:T(8,128)(2,1)} %param.17) | copy-start | bytes 12292
  29.2 7.3 %collective-permute-start.8 = (f32[64,256]{1,0:T(8,128)S(1)}, f32[64,256]{1,0:T(8,128)S(1)}, u32[]{:S(2)}, u32[]{:S(2)}) collective-permute-start(f32[64,256]{1,0:T(8,128)S(1)} %get-tuple-element.31), channel_id=1, source_target_pairs={{0,1},{1,0},{2,3},{3,2},{4,5},{5,4},{6,7},{7,6},{8,9},{9,8},{10,11... | collective-permute-start | bytes 196616 | tf_op jit(solution)/shard_map/ppermute | solution.py:293
  35.2 4.6 %collective-permute-start.9 = (f32[64,256]{1,0:T(8,128)S(1)}, f32[64,256]{1,0:T(8,128)S(1)}, u32[]{:S(2)}, u32[]{:S(2)}) collective-permute-start(f32[64,256]{1,0:T(8,128)S(1)} %get-tuple-element.32), channel_id=1, source_target_pairs={{1,2},{3,4},{5,6},{7,8},{9,10},{11,12},{13,14},{0,16},{15,31},{17,... | collective-permute-start | bytes 196616 | tf_op jit(solution)/shard_map/ppermute | solution.py:303
